TPU v7x, 32 devices: a whole 2x2x4 slice. The times are simulated.
32 devices in a mesh: groups: 2 (over x), node: 8 (over z, y), rep: 2 (over core).
Axes of the slice: x: 2, y: 2, z: 4, core: 2. Of those that a mesh axis runs over, the one named last changes fastest.
Arguments:
- normed_input: bfloat16 [4, 1024, 5120], P(('groups', 'rep'), 'node'), parts along dimension 0, may hold values from -6 to 6
- queries: bfloat16 [4, 1024, 2560], P(('groups', 'rep'), 'node'), parts along dimension 0, may hold values from -120 to 120
- rotated_key_heads: bfloat16 [4, 1024, 512], P(('groups', 'rep'), 'node'), parts along dimension 0, may hold values from -6 to 6
- frozen_value_rows: bfloat16 [4, 1024, 512], P(('groups', 'rep'), 'node'), parts along dimension 0, may hold values from -6 to 6
- adapter_down_weight: bfloat16 [5120, 32], replicated, may hold values from -0.078125 to 0.078125
- adapter_up_weight: bfloat16 [32, 512], replicated, may hold values from -1 to 1
- output_gradient: bfloat16 [4, 1024, 2560], P(('groups', 'rep'), 'node'), parts along dimension 0, may hold values from -6 to 6
- parents: int32 [4, 8], P(('groups', 'rep')), parts along dimension 0, may hold values from -1 to 6, as said below
- lengths: int32 [4, 8], P(('groups', 'rep')), parts along dimension 0, may hold values from 32 to 128, as said below
Outputs:
- attended: bfloat16 [4, 1024, 2560], P(('groups', 'rep'), 'node'), parts along dimension 0
- query_grad: bfloat16 [4, 1024, 2560], P(('groups', 'rep'), 'node'), parts along dimension 0
- down_grad: float32 [10240, 32], P('groups'), parts along dimension 0
- up_grad: float32 [64, 512], P('groups'), parts along dimension 0
There are 2 independent parts, one for each index of `groups`. A program takes and returns all parts, laid end to end along the dimension named above; an argument that names none is the same for every part. Nothing has to cross between parts.
Inputs may be any that keep to these rules, and one draw needn't show every extreme that they name: `parents`: slots 0 to 1 form the shared prompt, each the parent of the next, slot 0 the root. Every other slot's parent is slot 1 or a slot below it, and every ancestor of a slot s outside the prompt lies among the slots s - 5 to s - 1. `lengths`: prompt blocks are full.
All inputs are finite; a program needn't handle non-finite values.
Results may differ from a plain program's by a relative error of at most 0.0062.
Values may be sent and summed in bfloat16 or wider, within the bound.
No kernel may reach another device: no remote copies, remote signals or barrier semaphores. Data moves between devices by JAX's collectives and lax.ppermute only.
A program may use at most 128 MiB of HBM per device.

v0:
```python
import functools

import jax
import jax.numpy as jnp
from jax import lax
from jax.experimental import pallas as pl
from jax.experimental.pallas import tpu as pltpu
from jax.sharding import PartitionSpec as P


HQ = 20
KEY_HEADS = 4
HEAD_SIZE = 128
PROMPT = 2
SPAN = 5
PER = HQ // KEY_HEADS

NEGATIVE = -1e30
LOG2E = 1.4426950408889634
F32 = jnp.float32
BF16 = jnp.bfloat16


VMEM_LIMIT = 56 * 1024 * 1024


def dot(a, b):
    return lax.dot_general(a, b, (((1,), (0,)), ((), ())), preferred_element_type=F32)


def dot_nt(a, b):
    return lax.dot_general(a, b, (((1,), (1,)), ((), ())), preferred_element_type=F32)


def dot_tn(a, b):
    return lax.dot_general(a, b, (((0,), (0,)), ((), ())), preferred_element_type=F32)


def paired(slots):
    return slots % 2 == 0 and slots <= 1 + PROMPT + SPAN


def candidate_count(slots):
    return slots if paired(slots) else 1 + PROMPT + SPAN


def candidate_slot(slots, own, c):
    if paired(slots):
        pair = own - (c // 2) * 2
        slot = pair + (c % 2) * (1 - 2 * (pair % 2))
        return jnp.where(pair >= 0, slot, -1)
    window = own - c
    window = jnp.where(window >= PROMPT, window, -1)
    prompt = c - SPAN - 1
    prompt = jnp.where(prompt < own, prompt, -1)
    return jnp.where(c == 0, own, jnp.where(c <= SPAN, window, prompt))


def mark_candidates(slots, parents_ref, lengths_ref, live_ref):
    own = lax.axis_index("node")
    count = candidate_count(slots)
    for c in range(count):
        live_ref[c] = 0
    live_ref[0] = lengths_ref[0, own]

    def climb(step, current):
        at = jnp.maximum(current, 0)
        for c in range(1, count):
            slot = candidate_slot(slots, own, c)

            @pl.when((slot == current) & (current >= 0))
            def _():
                live_ref[c] = lengths_ref[0, at]

        return jnp.where(current >= 0, parents_ref[0, at], -1)

    lax.fori_loop(0, PROMPT + SPAN, climb, parents_ref[0, own])


def prepare_kernel(
    lengths_ref, x_ref, down_ref, up_ref, frozen_ref, q_ref, g_ref,
    message_ref, qt_ref, gt_ref, gs_ref,
):
    own = lax.axis_index("node")
    rows = x_ref.shape[0]
    width = frozen_ref.shape[1]
    low_t = dot_nt(down_ref[...], x_ref[...]).astype(BF16)
    values = frozen_ref[...].astype(F32) + dot_tn(low_t, up_ref[...])
    message_ref[:rows, :] = values.astype(BF16)
    half = low_t.shape[0] // 2
    message_ref[rows:, :] = jnp.zeros((half, width), BF16)
    message_ref[rows:, :rows] = low_t[:half]
    message_ref[rows:, rows : 2 * rows] = low_t[half:]
    length = lengths_ref[0, own]
    live = lax.broadcasted_iota(jnp.int32, (rows, HEAD_SIZE), 0) < length
    for h in range(HQ):
        cols = slice(h * HEAD_SIZE, (h + 1) * HEAD_SIZE)
        here = slice(h * rows, (h + 1) * rows)
        qt_ref[:, here] = q_ref[:, cols].T
        g = jnp.where(live, g_ref[:, cols].astype(F32), 0.0).astype(BF16)
        gs_ref[here, :] = g
        gt_ref[:, here] = g.T


def prepare(lengths, x, down_t, up, frozen, q, g):
    rows = x.shape[0]
    rank, width = up.shape
    vm = pl.BlockSpec(memory_space=pltpu.VMEM)
    return pl.pallas_call(
        prepare_kernel,
        name="prepare",
        out_shape=(
            jax.ShapeDtypeStruct((rows + rank // 2, width), BF16),
            jax.ShapeDtypeStruct((HEAD_SIZE, HQ * rows), BF16),
            jax.ShapeDtypeStruct((HEAD_SIZE, HQ * rows), BF16),
            jax.ShapeDtypeStruct((HQ * rows, HEAD_SIZE), BF16),
        ),
        in_specs=[pl.BlockSpec(memory_space=pltpu.SMEM)] + [vm] * 6,
        out_specs=(vm,) * 4,
        compiler_params=pltpu.CompilerParams(vmem_limit_bytes=VMEM_LIMIT),
        cost_estimate=pl.CostEstimate(flops=100_000_000, bytes_accessed=6_000_000, transcendentals=0),
    )(lengths, x, down_t, up, frozen, q, g)


def fill_bias(live_ref, bias_ref):
    rows = bias_ref.shape[1]
    key_at = lax.broadcasted_iota(jnp.int32, (rows, rows), 0)
    query_at = lax.broadcasted_iota(jnp.int32, (rows, rows), 1)
    for c in range(live_ref.shape[0]):
        allowed = key_at < live_ref[c]
        if c == 0:
            allowed &= key_at <= query_at
        bias_ref[c] = jnp.where(allowed, 0.0, NEGATIVE)


def stats_kernel(slots, scale, *refs):
    count = candidate_count(slots)
    parents_ref, lengths_ref = refs[:2]
    key_refs = refs[2 : 2 + count]
    qt_ref, gs_ref, up_ref = refs[2 + count : 5 + count]
    proj_ref, part_ref, lse_ref = refs[5 + count : 8 + count]
    live_ref, keys, weights, bias, tops, acc = refs[8 + count :]
    group = pl.program_id(0)
    rows = key_refs[0].shape[0]
    own = lax.axis_index("node")

    @pl.when(group == 0)
    def _():
        mark_candidates(slots, parents_ref, lengths_ref, live_ref)
        fill_bias(live_ref, bias)
        acc[...] = jnp.zeros_like(acc)

    for c in range(count):
        keys[c * rows : (c + 1) * rows] = key_refs[c][...]
    top = [None] * PER
    total = [None] * PER
    for j in range(0, count, 2):
        pair = slice(j * rows, (j + 2) * rows)
        for h in range(PER):
            here = slice(h * rows, (h + 1) * rows)
            s = dot(keys[pair], qt_ref[:, here])
            s = jnp.concatenate([s[:rows] + bias[j], s[rows:] + bias[j + 1]], axis=0)
            high = jnp.max(s, axis=0, keepdims=True) * scale
            raised = high if j == 0 else jnp.maximum(top[h], high)
            p = jnp.exp2(s * scale - raised)
            weights[pair, here] = p
            tops[j // 2 : j // 2 + 1, here] = raised
            summed = jnp.sum(p, axis=0, keepdims=True)
            total[h] = summed if j == 0 else total[h] * jnp.exp2(top[h] - raised) + summed
            top[h] = raised
    for h in range(PER):
        here = slice(h * rows, (h + 1) * rows)
        lse_ref[:, here] = top[h] + jnp.log2(total[h])
    inverse = [1.0 / total[h] for h in range(PER)]
    up = up_ref[...]
    gs = gs_ref[...]
    for j in range(0, count, 2):
        pair = slice(j * rows, (j + 2) * rows)
        scaled = []
        for h in range(PER):
            here = slice(h * rows, (h + 1) * rows)
            factor = jnp.exp2(tops[j // 2 : j // 2 + 1, here] - top[h]) * inverse[h]
            scaled.append((weights[pair, here] * factor).astype(BF16))
        part = dot(jnp.concatenate(scaled, axis=1), gs)
        high = part.astype(BF16)
        rest = (part - high.astype(F32)).astype(BF16)
        proj = dot_nt(up, high) + dot_nt(up, rest)
        for c in (j, j + 1):
            half = slice((c - j) * rows, (c - j + 1) * rows)
            part_ref[c] = high[half]
            acc[c] += proj[:, half]

    @pl.when(group == pl.num_programs(0) - 1)
    def _():
        proj_ref[...] = jnp.zeros_like(proj_ref)
        for c in range(count):

            @pl.when(live_ref[c] > 0)
            def _():
                proj_ref[candidate_slot(slots, own, c)] = acc[c]


def stats(slots, parents, lengths, key_blocks, qt, gs, up):
    count = candidate_count(slots)
    rows, width = key_blocks[0].shape
    rank = up.shape[0]
    lanes = PER * rows
    scale = LOG2E * HEAD_SIZE ** (-0.5)
    smem = pl.BlockSpec(memory_space=pltpu.SMEM)
    column = pl.BlockSpec((rows, HEAD_SIZE), lambda k: (0, k))
    return pl.pallas_call(
        functools.partial(stats_kernel, slots, scale),
        name="stats",
        grid=(KEY_HEADS,),
        out_shape=(
            jax.ShapeDtypeStruct((slots, rank, rows), F32),
            jax.ShapeDtypeStruct((count, rows, width), BF16),
            jax.ShapeDtypeStruct((1, HQ * rows), F32),
        ),
        in_specs=[smem, smem]
        + [column] * count
        + [
            pl.BlockSpec((HEAD_SIZE, lanes), lambda k: (0, k)),
            pl.BlockSpec((lanes, HEAD_SIZE), lambda k: (k, 0)),
            pl.BlockSpec((rank, HEAD_SIZE), lambda k: (0, k)),
        ],
        out_specs=(
            pl.BlockSpec((slots, rank, rows), lambda k: (0, 0, 0)),
            pl.BlockSpec((count, rows, HEAD_SIZE), lambda k: (0, 0, k)),
            pl.BlockSpec((1, lanes), lambda k: (0, k)),
        ),
        scratch_shapes=[
            pltpu.SMEM((count,), jnp.int32),
            pltpu.VMEM((count * rows, HEAD_SIZE), BF16),
            pltpu.VMEM((count * rows, lanes), F32),
            pltpu.VMEM((count, rows, rows), F32),
            pltpu.VMEM((8, lanes), F32),
            pltpu.VMEM((count, rank, rows), F32),
        ],
        compiler_params=pltpu.CompilerParams(vmem_limit_bytes=VMEM_LIMIT, dimension_semantics=("arbitrary",)),
        cost_estimate=pl.CostEstimate(flops=2_000_000_000, bytes_accessed=5_000_000, transcendentals=3_000_000),
    )(parents, lengths, *key_blocks, qt, gs, up)


def attend_kernel(slots, scale, inverse_root, *refs):
    count = candidate_count(slots)
    parents_ref, lengths_ref = refs[:2]
    key_refs = refs[2 : 2 + count]
    value_refs = refs[2 + count : 2 + 2 * count]
    qt_ref, gt_ref, lse_ref = refs[2 + 2 * count : 5 + 2 * count]
    attended_ref, query_grad_ref = refs[-10:-8]
    live_ref, keys, values, weights, rounded, slopes, bias, out_t = refs[-8:]
    rows = key_refs[0].shape[0]
    own = lax.axis_index("node")
    mark_candidates(slots, parents_ref, lengths_ref, live_ref)
    fill_bias(live_ref, bias)
    for c in range(count):
        block = slice(c * rows, (c + 1) * rows)
        keys[block] = key_refs[c][...]
        values[block] = value_refs[c][...]
    for j in range(0, count, 2):
        pair = slice(j * rows, (j + 2) * rows)
        for h in range(PER):
            here = slice(h * rows, (h + 1) * rows)
            s = dot(keys[pair], qt_ref[:, here])
            s = jnp.concatenate([s[:rows] + bias[j], s[rows:] + bias[j + 1]], axis=0)
            w = jnp.exp2(s * scale - lse_ref[:, here])
            weights[pair, here] = w
            rounded[pair, here] = w.astype(BF16)
    values_t = values[...].T
    keys_t = keys[...].T
    dots = []
    for h in range(PER):
        here = slice(h * rows, (h + 1) * rows)
        out = dot(values_t, rounded[:, here])
        out_t[:, here] = out
        dots.append(jnp.sum(gt_ref[:, here].astype(F32) * out, axis=0, keepdims=True))
    for j in range(0, count, 2):
        pair = slice(j * rows, (j + 2) * rows)
        for h in range(PER):
            here = slice(h * rows, (h + 1) * rows)
            pressure = dot(values[pair], gt_ref[:, here])
            slopes[pair, here] = (weights[pair, here] * (pressure - dots[h]) * inverse_root).astype(BF16)
    live = lax.broadcasted_iota(jnp.int32, (rows, HEAD_SIZE), 0) < lengths_ref[0, own]
    for h in range(PER):
        cols = slice(h * HEAD_SIZE, (h + 1) * HEAD_SIZE)
        here = slice(h * rows, (h + 1) * rows)
        query_grad_ref[:, cols] = dot(keys_t, slopes[:, here]).T.astype(BF16)
        attended_ref[:, cols] = jnp.where(live, out_t[:, here].T, 0.0).astype(BF16)


def attend(slots, group, carried, parents, lengths, key_blocks, value_blocks, qt, gt, lse):
    count = candidate_count(slots)
    rows = key_blocks[0].shape[0]
    lanes = PER * rows
    inverse_root = HEAD_SIZE ** (-0.5)
    smem = pl.BlockSpec(memory_space=pltpu.SMEM)
    column = pl.BlockSpec((rows, HEAD_SIZE), lambda i: (0, group))
    wide = pl.BlockSpec((HEAD_SIZE, lanes), lambda i: (0, group))
    out = pl.BlockSpec((rows, PER * HEAD_SIZE), lambda i: (0, group))
    first = 5 + 2 * count
    return pl.pallas_call(
        functools.partial(attend_kernel, slots, LOG2E * inverse_root, inverse_root),
        name="attend",
        grid=(1,),
        out_shape=(jax.ShapeDtypeStruct((rows, HQ * HEAD_SIZE), BF16),) * 2,
        in_specs=[smem, smem]
        + [column] * (2 * count)
        + [wide, wide, pl.BlockSpec((1, lanes), lambda i: (0, group))]
        + [pl.BlockSpec(memory_space=pl.ANY)] * len(carried),
        out_specs=(out, out),
        scratch_shapes=[
            pltpu.SMEM((count,), jnp.int32),
            pltpu.VMEM((count * rows, HEAD_SIZE), BF16),
            pltpu.VMEM((count * rows, HEAD_SIZE), BF16),
            pltpu.VMEM((count * rows, lanes), F32),
            pltpu.VMEM((count * rows, lanes), BF16),
            pltpu.VMEM((count * rows, lanes), BF16),
            pltpu.VMEM((count, rows, rows), F32),
            pltpu.VMEM((HEAD_SIZE, lanes), F32),
        ],
        input_output_aliases={first + i: i for i in range(len(carried))},
        compiler_params=pltpu.CompilerParams(vmem_limit_bytes=VMEM_LIMIT, dimension_semantics=("arbitrary",)),
        cost_estimate=pl.CostEstimate(flops=800_000_000, bytes_accessed=1_500_000, transcendentals=700_000),
    )(parents, lengths, *key_blocks, *value_blocks, qt, gt, lse, *carried)


def gradient_kernel(factor, received_ref, x_ref, part_ref, even_ref, odd_ref, keep_ref, send_ref):
    rows, width = x_ref.shape
    rank = received_ref.shape[1]
    core = lax.axis_index("rep")
    half = keep_ref.shape[1]
    start = width - half
    total = jnp.sum(received_ref[...], axis=0).astype(BF16)

    def place(ref, which):
        if which == 0:
            ref[...] = dot(total, x_ref[:, :half]) * factor
        else:
            ref[:, :start] = dot(total, x_ref[:, half:]) * factor

    for mine in range(2):

        @pl.when(core == mine)
        def _():
            place(send_ref, 1 - mine)
            place(keep_ref, mine)

    up = None
    for c in range(part_ref.shape[0]):
        slab = (odd_ref if c % 2 else even_ref)[(c // 2) * (rank // 2) : (c // 2 + 1) * (rank // 2), : 2 * rows]
        term = dot(jnp.concatenate([slab[:, :rows], slab[:, rows:]], axis=0), part_ref[c])
        up = term if up is None else up + term
    up = up * factor

    @pl.when(core == 0)
    def _():
        send_ref[:, start:] = up

    @pl.when(core == 1)
    def _():
        keep_ref[:, start:] = up


def gradients(received, x, parts, even, odd, factor):
    _, width = x.shape
    inner = parts.shape[2]
    rank = received.shape[1]
    half = (width + inner) // 2
    vm = pl.BlockSpec(memory_space=pltpu.VMEM)
    return pl.pallas_call(
        functools.partial(gradient_kernel, factor),
        name="gradients",
        out_shape=(jax.ShapeDtypeStruct((rank, half), F32),) * 2,
        in_specs=[vm] * 5,
        out_specs=(vm, vm),
        compiler_params=pltpu.CompilerParams(vmem_limit_bytes=VMEM_LIMIT),
        cost_estimate=pl.CostEstimate(flops=80_000_000, bytes_accessed=4_000_000, transcendentals=0),
    )(received, x, parts, even, odd)


def gather_blocks(slots, block):
    if not paired(slots):
        own = lax.axis_index("node")
        whole = lax.all_gather(block, "node")
        return [block] + [
            lax.dynamic_index_in_dim(whole, jnp.maximum(candidate_slot(slots, own, c), 0), 0, keepdims=False)
            for c in range(1, candidate_count(slots))
        ]
    swap = [(i, i ^ 1) for i in range(slots)]
    columns = [block]
    for d in range(2, slots, 2):
        columns.append(lax.ppermute(block, "node", [(i, i + d) for i in range(slots - d)]))
    blocks = []
    for column in columns:
        blocks += [column, lax.ppermute(column, "node", swap)]
    return blocks


def sum_over_all(slots, keep, send):
    core = lax.axis_index("rep")
    own = lax.axis_index("node")
    swap_core = [(0, 1), (1, 0)]

    def swap(x, bit):
        return lax.ppermute(x, "node", [(i, i ^ bit) for i in range(slots)])

    came = lax.ppermute(send, "rep", swap_core)
    total = keep + came
    quarter = total.shape[1] // 2
    low, high = total[:, :quarter], total[:, quarter:]
    odd = own % 2 == 1
    mine = jnp.where(odd, high, low)
    other = jnp.where(odd, low, high).astype(BF16)
    mine = (mine + swap(other, 1).astype(F32)).astype(BF16)
    bit = 2
    while bit < slots:
        mine = (mine.astype(F32) + swap(mine, bit).astype(F32)).astype(BF16)
        bit *= 2
    other = swap(mine, 1)
    half = jnp.concatenate([jnp.where(odd, other, mine), jnp.where(odd, mine, other)], axis=1)
    other = lax.ppermute(half, "rep", swap_core)
    second = core == 1
    whole = jnp.concatenate([jnp.where(second, other, half), jnp.where(second, half, other)], axis=1)
    return whole.astype(F32)


def on_device(
    normed_input,
    queries,
    rotated_key_heads,
    frozen_value_rows,
    adapter_down_weight,
    adapter_up_weight,
    output_gradient,
    parents,
    lengths,
):
    x = normed_input[0]
    rows, width = x.shape
    slots = lax.axis_size("node")
    key_blocks = gather_blocks(slots, rotated_key_heads[0])
    message, qt, gt, gs = prepare(
        lengths, x, adapter_down_weight.T, adapter_up_weight, frozen_value_rows[0], queries[0], output_gradient[0]
    )
    messages = gather_blocks(slots, message)
    projected, parts, lse = stats(slots, parents, lengths, key_blocks, qt, gs, adapter_up_weight)
    received = lax.all_to_all(projected, "node", 0, 0)
    factor = (slots * lax.axis_size("rep") * rows) ** (-0.5)
    slabs = [message[rows:] for message in messages]
    even = jnp.concatenate(slabs[0::2], axis=0)
    if paired(slots):
        odd = lax.ppermute(even, "node", [(i, i ^ 1) for i in range(slots)])
    else:
        odd = jnp.concatenate(slabs[1::2], axis=0)
    keep, send = gradients(received, x, parts, even, odd, factor)
    whole = sum_over_all(slots, keep, send)
    carried = ()
    for group in range(KEY_HEADS):
        carried = attend(slots, group, carried, parents, lengths, key_blocks, messages, qt, gt, lse)
    attended, query_grad = carried
    return (attended[None], query_grad[None], whole[:, :width].T, whole[:, width:])


def solution(mesh):
    tokens = P(("groups", "rep"), "node", None)
    trees = P(("groups", "rep"), None)
    return jax.shard_map(
        on_device,
        mesh=mesh,
        in_specs=(tokens,) * 4 + (P(), P()) + (tokens, trees, trees),
        out_specs=(tokens, tokens, P("groups", None), P("groups", None)),
        check_vma=False,
    )
```

profile of v0, /device:TPU:0, one launch (start us, length us, event | category | flops | bytes accessed | tf_op | source)
XLA Modules:
  0.0 104.1 jit_solution(1878471166431689239)
XLA Ops:
  0.6 7.0 %collective-permute-start.5 = (bf16[128,512]{1,0:T(8,128)(2,1)}, bf16[128,512]{1,0:T(8,128)(2,1)S(1)}, u32[]{:S(2)}, u32[]{:S(2)}) collective-permute-start(bf16[128,512]{1,0:T(8,128)(2,1)} %bitcast.14), channel_id=1, source_target_pairs={{0,12},{2,14},{1,13},{3,15},{16,28},{18,30},{17,29},{19,31}} | collective-permute-start | bytes 393224 | tf_op jit(solution)/shard_map/ppermute | solution.py:393
  7.6 1.3 %collective-permute-start.3 = (bf16[128,512]{1,0:T(8,128)(2,1)}, bf16[128,512]{1,0:T(8,128)(2,1)S(1)}, u32[]{:S(2)}, u32[]{:S(2)}) collective-permute-start(bf16[128,512]{1,0:T(8,128)(2,1)} %bitcast.15), channel_id=1, source_target_pairs={{0,8},{2,10},{4,12},{6,14},{1,9},{3,11},{5,13},{7,15},{16,24},{18,... | collective-permute-start | bytes 393224 | tf_op jit(solution)/shard_map/ppermute | solution.py:393
  8.9 2.5 %collective-permute-start.1 = (bf16[128,512]{1,0:T(8,128)(2,1)}, bf16[128,512]{1,0:T(8,128)(2,1)S(1)}, u32[]{:S(2)}, u32[]{:S(2)}) collective-permute-start(bf16[128,512]{1,0:T(8,128)(2,1)} %bitcast.16), channel_id=1, source_target_pairs={{0,4},{2,6},{4,8},{6,10},{8,12},{10,14},{1,5},{3,7},{5,9},{7,11},{... | collective-permute-start | bytes 393224 | tf_op jit(solution)/shard_map/ppermute | solution.py:393
  11.4 1.6 %collective-permute-start = (bf16[128,512]{1,0:T(8,128)(2,1)}, bf16[128,512]{1,0:T(8,128)(2,1)S(1)}, u32[]{:S(2)}, u32[]{:S(2)}) collective-permute-start(bf16[128,512]{1,0:T(8,128)(2,1)} %bitcast.17), channel_id=1, source_target_pairs={{0,2},{2,0},{4,6},{6,4},{8,10},{10,8},{12,14},{14,12},{1,3},{3,1},... | collective-permute-start | bytes 393224 | tf_op jit(solution)/shard_map/ppermute | solution.py:396
  13.5 1.1 %collective-permute-done.3.refs_6_ = bf16[128,512]{1,0:T(8,128)(2,1)S(1)} collective-permute-done((bf16[128,512]{1,0:T(8,128)(2,1)}, bf16[128,512]{1,0:T(8,128)(2,1)S(1)}, u32[]{:S(2)}, u32[]{:S(2)}) %collective-permute-start.3) | collective-permute-done | bytes 131104 | tf_op jit(solution)/shard_map/ppermute | solution.py:393
  14.7 1.5 %collective-permute-start.4 = (bf16[128,512]{1,0:T(8,128)(2,1)S(1)}, bf16[128,512]{1,0:T(8,128)(2,1)S(1)}, u32[]{:S(2)}, u32[]{:S(2)}) collective-permute-start(bf16[128,512]{1,0:T(8,128)(2,1)S(1)} %collective-permute-done.3.refs_6_), channel_id=1, source_target_pairs={{0,2},{2,0},{4,6},{6,4},{8,10},{10,8},{12,14},{14,12},{1,3},{3,1},... | collective-permute-start | bytes 393224 | tf_op jit(solution)/shard_map/ppermute | solution.py:396
  16.3 1.5 %collective-permute-start.2 = (bf16[128,512]{1,0:T(8,128)(2,1)S(1)}, bf16[128,512]{1,0:T(8,128)(2,1)S(1)}, u32[]{:S(2)}, u32[]{:S(2)}) collective-permute-start(bf16[128,512]{1,0:T(8,128)(2,1)S(1)} %collective-permute-done.1.refs_4_), channel_id=1, source_target_pairs={{0,2},{2,0},{4,6},{6,4},{8,10},{10,8},{12,14},{14,12},{1,3},{3,1},... | collective-permute-start | bytes 393224 | tf_op jit(solution)/shard_map/ppermute | solution.py:396
  17.9 3.9 %prepare.1 = (bf16[144,512]{1,0:T(8,128)(2,1)}, bf16[128,2560]{1,0:T(8,128)(2,1)}, bf16[128,2560]{1,0:T(8,128)(2,1)}, bf16[2560,128]{1,0:T(8,128)(2,1)}) custom-call(s32[1,8]{1,0:T(1,128)} %refs_1_.9, bf16[128,5120]{1,0:T(8,128)(2,1)} %bitcast.12, bf16[32,5120]{1,0:T(8,128)(2,1)} %bitcast.25, bf16[32,512]{1,0:T(8,128)(2,1)} %refs_12_.1, ...), custom_call_target="tpu_custom_call" | custom-call | flops 100000000 | bytes 6000000 | tf_op jit(solution)/shard_map/prepare/pallas_call | solution.py:109
  21.8 6.6 %collective-permute-start.12 = (bf16[144,512]{1,0:T(8,128)(2,1)}, bf16[144,512]{1,0:T(8,128)(2,1)S(1)}, u32[]{:S(2)}, u32[]{:S(2)}) collective-permute-start(bf16[144,512]{1,0:T(8,128)(2,1)} %get-tuple-element.21.refs_10_), channel_id=1, source_target_pairs={{0,12},{2,14},{1,13},{3,15},{16,28},{18,30},{17,29},{19,31}} | collective-permute-start | bytes 442376 | tf_op jit(solution)/shard_map/ppermute | solution.py:393
  28.4 2.0 %collective-permute-start.10 = (bf16[144,512]{1,0:T(8,128)(2,1)}, bf16[144,512]{1,0:T(8,128)(2,1)S(1)}, u32[]{:S(2)}, u32[]{:S(2)}) collective-permute-start(bf16[144,512]{1,0:T(8,128)(2,1)} %get-tuple-element.21.refs_10_), channel_id=1, source_target_pairs={{0,8},{2,10},{4,12},{6,14},{1,9},{3,11},{5,13},{7,15},{16,24},{18,... | collective-permute-start | bytes 442376 | tf_op jit(solution)/shard_map/ppermute | solution.py:393
  30.4 1.8 %collective-permute-start.8 = (bf16[144,512]{1,0:T(8,128)(2,1)}, bf16[144,512]{1,0:T(8,128)(2,1)S(1)}, u32[]{:S(2)}, u32[]{:S(2)}) collective-permute-start(bf16[144,512]{1,0:T(8,128)(2,1)} %get-tuple-element.21.refs_10_), channel_id=1, source_target_pairs={{0,4},{2,6},{4,8},{6,10},{8,12},{10,14},{1,5},{3,7},{5,9},{7,11},{... | collective-permute-start | bytes 442376 | tf_op jit(solution)/shard_map/ppermute | solution.py:393
  33.0 10.5 %stats.1 = (f32[8,32,128]{2,1,0:T(8,128)}, bf16[8,128,512]{2,1,0:T(8,128)(2,1)}, f32[1,2560]{1,0:T(1,128)}) custom-call(s32[1,8]{1,0:T(1,128)} %refs_0_.9, s32[1,8]{1,0:T(1,128)} %refs_1_.9, bf16[128,512]{1,0:T(8,128)(2,1)} %bitcast.18, bf16[128,512]{1,0:T(8,128)(2,1)} %copy-done.11, bf16[128,512]{1,0:T(8,128)(2,1)} %copy-done.10, ...), custom_call_target="tpu_custom_call" | custom-call | flops 2000000000 | bytes 5000000 | tf_op jit(solution)/shard_map/stats/pallas_call | solution.py:211
  43.4 3.4 %all-to-all-start = ((f32[8,32,128]{2,1,0:T(8,128)}), f32[8,32,128]{2,1,0:T(8,128)S(1)}, u32[]{:S(2)}, u32[]{:S(2)}) async-start(f32[8,32,128]{2,1,0:T(8,128)} %get-tuple-element.34), calls=%async_computation | async-start | bytes 262144 | tf_op jit(solution)/shard_map/all_to_all | solution.py:448
  47.0 2.0 %collective-permute-start.14 = (bf16[64,512]{1,0:T(8,128)(2,1)S(1)}, bf16[64,512]{1,0:T(8,128)(2,1)S(1)}, u32[]{:S(2)}, u32[]{:S(2)}) collective-permute-start(bf16[64,512]{1,0:T(8,128)(2,1)S(1)} %pad_maximum_fusion.1.even_ref), channel_id=1, source_target_pairs={{0,2},{2,0},{4,6},{6,4},{8,10},{10,8},{12,14},{14,12},{1,3},{3,1},... | collective-permute-start | bytes 196616 | tf_op jit(solution)/shard_map/ppermute | solution.py:453
  48.9 2.4 %collective-permute-done.14.odd_ref = bf16[64,512]{1,0:T(8,128)(2,1)S(1)} collective-permute-done((bf16[64,512]{1,0:T(8,128)(2,1)S(1)}, bf16[64,512]{1,0:T(8,128)(2,1)S(1)}, u32[]{:S(2)}, u32[]{:S(2)}) %collective-permute-start.14) | collective-permute-done | bytes 65568 | tf_op jit(solution)/shard_map/ppermute | solution.py:453
  51.4 2.7 %all-to-all-done.received_ref = f32[8,32,128]{2,1,0:T(8,128)S(1)} async-done(((f32[8,32,128]{2,1,0:T(8,128)}), f32[8,32,128]{2,1,0:T(8,128)S(1)}, u32[]{:S(2)}, u32[]{:S(2)}) %all-to-all-start) | async-done | bytes 131104 | tf_op jit(solution)/shard_map/all_to_all | solution.py:448
  54.8 3.2 %gradients.1 = (f32[32,2816]{1,0:T(8,128)}, f32[32,2816]{1,0:T(8,128)}) custom-call(f32[8,32,128]{2,1,0:T(8,128)} %copy-done.15, bf16[128,5120]{1,0:T(8,128)(2,1)} %bitcast.13, bf16[8,128,512]{2,1,0:T(8,128)(2,1)} %get-tuple-element.35.part_ref, bf16[64,512]{1,0:T(8,128)(2,1)} %copy-done.16, bf16[64,512]{1,0:T(8,128)(2,1)} %copy-done.17), custom_call_target="tpu_custom_call" | custom-call | flops 80000000 | bytes 4000000 | tf_op jit(solution)/shard_map/gradients/pallas_call | solution.py:371
  58.0 1.9 %collective-permute-done.15 = f32[32,2816]{1,0:T(8,128)S(1)} collective-permute-done((f32[32,2816]{1,0:T(8,128)}, f32[32,2816]{1,0:T(8,128)S(1)}, u32[]{:S(2)}, u32[]{:S(2)}) %collective-permute-start.15) | collective-permute-done | bytes 360480 | tf_op jit(solution)/shard_map/ppermute | solution.py:408
  59.9 1.0 add.17
  61.2 4.4 %collective-permute-done.16 = bf16[32,1408]{1,0:T(8,128)(2,1)S(1)} collective-permute-done((bf16[32,1408]{1,0:T(8,128)(2,1)S(1)}, bf16[32,1408]{1,0:T(8,128)(2,1)S(1)}, u32[]{:S(2)}, u32[]{:S(2)}) %collective-permute-start.16) | collective-permute-done | bytes 90144 | tf_op jit(solution)/shard_map/ppermute | solution.py:406
  65.7 4.5 %collective-permute-done.17 = bf16[32,1408]{1,0:T(8,128)(2,1)S(1)} collective-permute-done((bf16[32,1408]{1,0:T(8,128)(2,1)S(1)}, bf16[32,1408]{1,0:T(8,128)(2,1)S(1)}, u32[]{:S(2)}, u32[]{:S(2)}) %collective-permute-start.17) | collective-permute-done | bytes 90144 | tf_op jit(solution)/shard_map/ppermute | solution.py:406
  70.7 1.1 %collective-permute-start.7 = (bf16[144,512]{1,0:T(8,128)(2,1)S(1)}, bf16[144,512]{1,0:T(8,128)(2,1)S(1)}, u32[]{:S(2)}, u32[]{:S(2)}) collective-permute-start(bf16[144,512]{1,0:T(8,128)(2,1)S(1)} %copy-done), channel_id=1, source_target_pairs={{0,2},{2,0},{4,6},{6,4},{8,10},{10,8},{12,14},{14,12},{1,3},{3,1},... | collective-permute-start | bytes 442376 | tf_op jit(solution)/shard_map/ppermute | solution.py:396
  72.8 1.1 %collective-permute-start.11 = (bf16[144,512]{1,0:T(8,128)(2,1)S(1)}, bf16[144,512]{1,0:T(8,128)(2,1)S(1)}, u32[]{:S(2)}, u32[]{:S(2)}) collective-permute-start(bf16[144,512]{1,0:T(8,128)(2,1)S(1)} %collective-permute-done.10.refs_14_), channel_id=1, source_target_pairs={{0,2},{2,0},{4,6},{6,4},{8,10},{10,8},{12,14},{14,12},{1,3},{3,1},... | collective-permute-start | bytes 442376 | tf_op jit(solution)/shard_map/ppermute | solution.py:396
  74.8 1.4 %collective-permute-done.18 = bf16[32,1408]{1,0:T(8,128)(2,1)S(1)} collective-permute-done((bf16[32,1408]{1,0:T(8,128)(2,1)S(1)}, bf16[32,1408]{1,0:T(8,128)(2,1)S(1)}, u32[]{:S(2)}, u32[]{:S(2)}) %collective-permute-start.18) | collective-permute-done | bytes 90144 | tf_op jit(solution)/shard_map/ppermute | solution.py:406
  76.2 0.9 collective-permute-start.19
  77.5 3.2 %collective-permute-done.13.refs_17_ = bf16[144,512]{1,0:T(8,128)(2,1)S(1)} collective-permute-done((bf16[144,512]{1,0:T(8,128)(2,1)S(1)}, bf16[144,512]{1,0:T(8,128)(2,1)S(1)}, u32[]{:S(2)}, u32[]{:S(2)}) %collective-permute-start.13) | collective-permute-done | bytes 147488 | tf_op jit(solution)/shard_map/ppermute | solution.py:396
  80.6 2.6 %collective-permute-done.11.refs_15_ = bf16[144,512]{1,0:T(8,128)(2,1)S(1)} collective-permute-done((bf16[144,512]{1,0:T(8,128)(2,1)S(1)}, bf16[144,512]{1,0:T(8,128)(2,1)S(1)}, u32[]{:S(2)}, u32[]{:S(2)}) %collective-permute-start.11) | collective-permute-done | bytes 147488 | tf_op jit(solution)/shard_map/ppermute | solution.py:396
  83.2 1.6 %collective-permute-done.9.refs_13_ = bf16[144,512]{1,0:T(8,128)(2,1)S(1)} collective-permute-done((bf16[144,512]{1,0:T(8,128)(2,1)S(1)}, bf16[144,512]{1,0:T(8,128)(2,1)S(1)}, u32[]{:S(2)}, u32[]{:S(2)}) %collective-permute-start.9) | collective-permute-done | bytes 147488 | tf_op jit(solution)/shard_map/ppermute | solution.py:396
  85.5 4.2 %attend.4 = (bf16[128,2560]{1,0:T(8,128)(2,1)}, bf16[128,2560]{1,0:T(8,128)(2,1)}) custom-call(s32[1,8]{1,0:T(1,128)} %refs_0_.9, s32[1,8]{1,0:T(1,128)} %refs_1_.9, bf16[128,512]{1,0:T(8,128)(2,1)} %bitcast.19, bf16[128,512]{1,0:T(8,128)(2,1)} %copy-done.11, bf16[128,512]{1,0:T(8,128)(2,1)} %copy-done.10, bf16[128,512]{1,0:T(8,128)(2,1)} %copy-done.14, ...), custom_call_target="tpu_custom_call" | custom-call | flops 800000000 | bytes 1500000 | tf_op jit(solution)/shard_map/attend/pallas_call | solution.py:302
  89.8 4.2 %attend.5 = (bf16[128,2560]{1,0:T(8,128)(2,1)}, bf16[128,2560]{1,0:T(8,128)(2,1)}) custom-call(s32[1,8]{1,0:T(1,128)} %refs_0_.9, s32[1,8]{1,0:T(1,128)} %refs_1_.9, bf16[128,512]{1,0:T(8,128)(2,1)} %bitcast.20, bf16[128,512]{1,0:T(8,128)(2,1)} %copy-done.11, bf16[128,512]{1,0:T(8,128)(2,1)} %copy-done.10, ...), custom_call_target="tpu_custom_call", output_to_operand_aliasing={{0}: (21, {}), {1}: (22, {})} | custom-call | flops 800000000 | bytes 1500000 | tf_op jit(solution)/shard_map/attend/pallas_call | solution.py:302
  94.0 4.2 %attend.6 = (bf16[128,2560]{1,0:T(8,128)(2,1)}, bf16[128,2560]{1,0:T(8,128)(2,1)}) custom-call(s32[1,8]{1,0:T(1,128)} %refs_0_.9, s32[1,8]{1,0:T(1,128)} %refs_1_.9, bf16[128,512]{1,0:T(8,128)(2,1)} %bitcast.21, bf16[128,512]{1,0:T(8,128)(2,1)} %copy-done.11, bf16[128,512]{1,0:T(8,128)(2,1)} %copy-done.10, ...), custom_call_target="tpu_custom_call", output_to_operand_aliasing={{0}: (21, {}), {1}: (22, {})} | custom-call | flops 800000000 | bytes 1500000 | tf_op jit(solution)/shard_map/attend/pallas_call | solution.py:302
  98.3 4.2 %attend.7 = (bf16[128,2560]{1,0:T(8,128)(2,1)}, bf16[128,2560]{1,0:T(8,128)(2,1)}) custom-call(s32[1,8]{1,0:T(1,128)} %refs_0_.9, s32[1,8]{1,0:T(1,128)} %refs_1_.9, bf16[128,512]{1,0:T(8,128)(2,1)} %bitcast.22, bf16[128,512]{1,0:T(8,128)(2,1)} %copy-done.11, bf16[128,512]{1,0:T(8,128)(2,1)} %copy-done.10, ...), custom_call_target="tpu_custom_call", output_to_operand_aliasing={{0}: (21, {}), {1}: (22, {})} | custom-call | flops 800000000 | bytes 1500000 | tf_op jit(solution)/shard_map/attend/pallas_call | solution.py:302
  (71 shorter events, 7.5 us)
Async XLA Ops:
  0.6 12.4 %collective-permute-start.5 = (bf16[128,512]{1,0:T(8,128)(2,1)}, bf16[128,512]{1,0:T(8,128)(2,1)S(1)}, u32[]{:S(2)}, u32[]{:S(2)}) collective-permute-start(bf16[128,512]{1,0:T(8,128)(2,1)} %bitcast.14), channel_id=1, source_target_pairs={{0,12},{2,14},{1,13},{3,15},{16,28},{18,30},{17,29},{19,31}} | collective-permute-start | bytes 393224 | tf_op jit(solution)/shard_map/ppermute | solution.py:393
  7.6 7.0 %collective-permute-start.3 = (bf16[128,512]{1,0:T(8,128)(2,1)}, bf16[128,512]{1,0:T(8,128)(2,1)S(1)}, u32[]{:S(2)}, u32[]{:S(2)}) collective-permute-start(bf16[128,512]{1,0:T(8,128)(2,1)} %bitcast.15), channel_id=1, source_target_pairs={{0,8},{2,10},{4,12},{6,14},{1,9},{3,11},{5,13},{7,15},{16,24},{18,... | collective-permute-start | bytes 393224 | tf_op jit(solution)/shard_map/ppermute | solution.py:393
  8.9 7.4 %collective-permute-start.1 = (bf16[128,512]{1,0:T(8,128)(2,1)}, bf16[128,512]{1,0:T(8,128)(2,1)S(1)}, u32[]{:S(2)}, u32[]{:S(2)}) collective-permute-start(bf16[128,512]{1,0:T(8,128)(2,1)} %bitcast.16), channel_id=1, source_target_pairs={{0,4},{2,6},{4,8},{6,10},{8,12},{10,14},{1,5},{3,7},{5,9},{7,11},{... | collective-permute-start | bytes 393224 | tf_op jit(solution)/shard_map/ppermute | solution.py:393
  11.4 17.0 %collective-permute-start = (bf16[128,512]{1,0:T(8,128)(2,1)}, bf16[128,512]{1,0:T(8,128)(2,1)S(1)}, u32[]{:S(2)}, u32[]{:S(2)}) collective-permute-start(bf16[128,512]{1,0:T(8,128)(2,1)} %bitcast.17), channel_id=1, source_target_pairs={{0,2},{2,0},{4,6},{6,4},{8,10},{10,8},{12,14},{14,12},{1,3},{3,1},... | collective-permute-start | bytes 393224 | tf_op jit(solution)/shard_map/ppermute | solution.py:396
  13.0 8.7 %copy-start.8 = (bf16[128,512]{1,0:T(8,128)(2,1)}, bf16[128,512]{1,0:T(8,128)(2,1)S(1)}, u32[]{:S(2)}) copy-start(bf16[128,512]{1,0:T(8,128)(2,1)S(1)} %collective-permute-done.5.refs_8_) | copy-start | bytes 393220
  13.0 17.4 %collective-permute-start.6 = (bf16[128,512]{1,0:T(8,128)(2,1)S(1)}, bf16[128,512]{1,0:T(8,128)(2,1)S(1)}, u32[]{:S(2)}, u32[]{:S(2)}) collective-permute-start(bf16[128,512]{1,0:T(8,128)(2,1)S(1)} %collective-permute-done.5.refs_8_), channel_id=1, source_target_pairs={{0,2},{2,0},{4,6},{6,4},{8,10},{10,8},{12,14},{14,12},{1,3},{3,1},... | collective-permute-start | bytes 393224 | tf_op jit(solution)/shard_map/ppermute | solution.py:396
  14.7 7.1 %copy-start.9 = (bf16[128,512]{1,0:T(8,128)(2,1)}, bf16[128,512]{1,0:T(8,128)(2,1)S(1)}, u32[]{:S(2)}) copy-start(bf16[128,512]{1,0:T(8,128)(2,1)S(1)} %collective-permute-done.3.refs_6_) | copy-start | bytes 393220
  14.7 17.6 %collective-permute-start.4 = (bf16[128,512]{1,0:T(8,128)(2,1)S(1)}, bf16[128,512]{1,0:T(8,128)(2,1)S(1)}, u32[]{:S(2)}, u32[]{:S(2)}) collective-permute-start(bf16[128,512]{1,0:T(8,128)(2,1)S(1)} %collective-permute-done.3.refs_6_), channel_id=1, source_target_pairs={{0,2},{2,0},{4,6},{6,4},{8,10},{10,8},{12,14},{14,12},{1,3},{3,1},... | collective-permute-start | bytes 393224 | tf_op jit(solution)/shard_map/ppermute | solution.py:396
  16.3 5.4 %copy-start.10 = (bf16[128,512]{1,0:T(8,128)(2,1)}, bf16[128,512]{1,0:T(8,128)(2,1)S(1)}, u32[]{:S(2)}) copy-start(bf16[128,512]{1,0:T(8,128)(2,1)S(1)} %collective-permute-done.1.refs_4_) | copy-start | bytes 393220
  16.3 15.9 %collective-permute-start.2 = (bf16[128,512]{1,0:T(8,128)(2,1)S(1)}, bf16[128,512]{1,0:T(8,128)(2,1)S(1)}, u32[]{:S(2)}, u32[]{:S(2)}) collective-permute-start(bf16[128,512]{1,0:T(8,128)(2,1)S(1)} %collective-permute-done.1.refs_4_), channel_id=1, source_target_pairs={{0,2},{2,0},{4,6},{6,4},{8,10},{10,8},{12,14},{14,12},{1,3},{3,1},... | collective-permute-start | bytes 393224 | tf_op jit(solution)/shard_map/ppermute | solution.py:396
  21.8 25.1 %collective-permute-start.12 = (bf16[144,512]{1,0:T(8,128)(2,1)}, bf16[144,512]{1,0:T(8,128)(2,1)S(1)}, u32[]{:S(2)}, u32[]{:S(2)}) collective-permute-start(bf16[144,512]{1,0:T(8,128)(2,1)} %get-tuple-element.21.refs_10_), channel_id=1, source_target_pairs={{0,12},{2,14},{1,13},{3,15},{16,28},{18,30},{17,29},{19,31}} | collective-permute-start | bytes 442376 | tf_op jit(solution)/shard_map/ppermute | solution.py:393
  28.4 18.4 %collective-permute-start.10 = (bf16[144,512]{1,0:T(8,128)(2,1)}, bf16[144,512]{1,0:T(8,128)(2,1)S(1)}, u32[]{:S(2)}, u32[]{:S(2)}) collective-permute-start(bf16[144,512]{1,0:T(8,128)(2,1)} %get-tuple-element.21.refs_10_), channel_id=1, source_target_pairs={{0,8},{2,10},{4,12},{6,14},{1,9},{3,11},{5,13},{7,15},{16,24},{18,... | collective-permute-start | bytes 442376 | tf_op jit(solution)/shard_map/ppermute | solution.py:393
  30.4 16.5 %collective-permute-start.8 = (bf16[144,512]{1,0:T(8,128)(2,1)}, bf16[144,512]{1,0:T(8,128)(2,1)S(1)}, u32[]{:S(2)}, u32[]{:S(2)}) collective-permute-start(bf16[144,512]{1,0:T(8,128)(2,1)} %get-tuple-element.21.refs_10_), channel_id=1, source_target_pairs={{0,4},{2,6},{4,8},{6,10},{8,12},{10,14},{1,5},{3,7},{5,9},{7,11},{... | collective-permute-start | bytes 442376 | tf_op jit(solution)/shard_map/ppermute | solution.py:393
  32.9 13.9 %copy-start = (bf16[144,512]{1,0:T(8,128)(2,1)S(1)}, bf16[144,512]{1,0:T(8,128)(2,1)}, u32[]{:S(2)}) copy-start(bf16[144,512]{1,0:T(8,128)(2,1)} %get-tuple-element.21.refs_10_) | copy-start | bytes 442372
  43.4 10.7 %all-to-all-start = ((f32[8,32,128]{2,1,0:T(8,128)}), f32[8,32,128]{2,1,0:T(8,128)S(1)}, u32[]{:S(2)}, u32[]{:S(2)}) async-start(f32[8,32,128]{2,1,0:T(8,128)} %get-tuple-element.34), calls=%async_computation | async-start | bytes 262144 | tf_op jit(solution)/shard_map/all_to_all | solution.py:448
  46.9 25.0 %copy-start.1 = (bf16[144,512]{1,0:T(8,128)(2,1)}, bf16[144,512]{1,0:T(8,128)(2,1)S(1)}, u32[]{:S(2)}) copy-start(bf16[144,512]{1,0:T(8,128)(2,1)S(1)} %collective-permute-done.12.refs_16_) | copy-start | bytes 442372
  46.9 25.9 %copy-start.2 = (bf16[144,512]{1,0:T(8,128)(2,1)}, bf16[144,512]{1,0:T(8,128)(2,1)S(1)}, u32[]{:S(2)}) copy-start(bf16[144,512]{1,0:T(8,128)(2,1)S(1)} %collective-permute-done.10.refs_14_) | copy-start | bytes 442372
  46.9 27.0 %copy-start.3 = (bf16[144,512]{1,0:T(8,128)(2,1)}, bf16[144,512]{1,0:T(8,128)(2,1)S(1)}, u32[]{:S(2)}) copy-start(bf16[144,512]{1,0:T(8,128)(2,1)S(1)} %collective-permute-done.8.refs_12_) | copy-start | bytes 442372
  47.0 7.2 %copy-start.16 = (bf16[64,512]{1,0:T(8,128)(2,1)}, bf16[64,512]{1,0:T(8,128)(2,1)S(1)}, u32[]{:S(2)}) copy-start(bf16[64,512]{1,0:T(8,128)(2,1)S(1)} %pad_maximum_fusion.1.even_ref) | copy-start | bytes 196612
  47.0 4.4 %collective-permute-start.14 = (bf16[64,512]{1,0:T(8,128)(2,1)S(1)}, bf16[64,512]{1,0:T(8,128)(2,1)S(1)}, u32[]{:S(2)}, u32[]{:S(2)}) collective-permute-start(bf16[64,512]{1,0:T(8,128)(2,1)S(1)} %pad_maximum_fusion.1.even_ref), channel_id=1, source_target_pairs={{0,2},{2,0},{4,6},{6,4},{8,10},{10,8},{12,14},{14,12},{1,3},{3,1},... | collective-permute-start | bytes 196616 | tf_op jit(solution)/shard_map/ppermute | solution.py:453
  58.0 1.9 %collective-permute-start.15 = (f32[32,2816]{1,0:T(8,128)}, f32[32,2816]{1,0:T(8,128)S(1)}, u32[]{:S(2)}, u32[]{:S(2)}) collective-permute-start(f32[32,2816]{1,0:T(8,128)} %get-tuple-element.37), channel_id=1, source_target_pairs={{0,1},{1,0},{2,3},{3,2},{4,5},{5,4},{6,7},{7,6},{8,9},{9,8},{10,11... | collective-permute-start | bytes 1081352 | tf_op jit(solution)/shard_map/ppermute | solution.py:408
  60.9 4.7 %collective-permute-start.16 = (bf16[32,1408]{1,0:T(8,128)(2,1)S(1)}, bf16[32,1408]{1,0:T(8,128)(2,1)S(1)}, u32[]{:S(2)}, u32[]{:S(2)}) collective-permute-start(bf16[32,1408]{1,0:T(8,128)(2,1)S(1)} %select_convert_fusion), channel_id=1, source_target_pairs={{0,2},{2,0},{4,6},{6,4},{8,10},{10,8},{12,14},{14,12},{1,3},{3,1},... | collective-permute-start | bytes 270344 | tf_op jit(solution)/shard_map/ppermute | solution.py:406
  65.7 4.6 %collective-permute-start.17 = (bf16[32,1408]{1,0:T(8,128)(2,1)S(1)}, bf16[32,1408]{1,0:T(8,128)(2,1)S(1)}, u32[]{:S(2)}, u32[]{:S(2)}) collective-permute-start(bf16[32,1408]{1,0:T(8,128)(2,1)S(1)} %add_convert_fusion.2), channel_id=1, source_target_pairs={{0,4},{2,6},{4,0},{6,2},{8,12},{10,14},{12,8},{14,10},{1,5},{3,7},... | collective-permute-start | bytes 270344 | tf_op jit(solution)/shard_map/ppermute | solution.py:406
  70.3 5.9 %collective-permute-start.18 = (bf16[32,1408]{1,0:T(8,128)(2,1)S(1)}, bf16[32,1408]{1,0:T(8,128)(2,1)S(1)}, u32[]{:S(2)}, u32[]{:S(2)}) collective-permute-start(bf16[32,1408]{1,0:T(8,128)(2,1)S(1)} %add_convert_fusion.1), channel_id=1, source_target_pairs={{0,8},{2,10},{4,12},{6,14},{8,0},{10,2},{12,4},{14,6},{1,9},{3,11}... | collective-permute-start | bytes 270344 | tf_op jit(solution)/shard_map/ppermute | solution.py:406
  70.7 6.7 %collective-permute-start.7 = (bf16[144,512]{1,0:T(8,128)(2,1)S(1)}, bf16[144,512]{1,0:T(8,128)(2,1)S(1)}, u32[]{:S(2)}, u32[]{:S(2)}) collective-permute-start(bf16[144,512]{1,0:T(8,128)(2,1)S(1)} %copy-done), channel_id=1, source_target_pairs={{0,2},{2,0},{4,6},{6,4},{8,10},{10,8},{12,14},{14,12},{1,3},{3,1},... | collective-permute-start | bytes 442376 | tf_op jit(solution)/shard_map/ppermute | solution.py:396
  71.9 8.8 %collective-permute-start.13 = (bf16[144,512]{1,0:T(8,128)(2,1)S(1)}, bf16[144,512]{1,0:T(8,128)(2,1)S(1)}, u32[]{:S(2)}, u32[]{:S(2)}) collective-permute-start(bf16[144,512]{1,0:T(8,128)(2,1)S(1)} %collective-permute-done.12.refs_16_), channel_id=1, source_target_pairs={{0,2},{2,0},{4,6},{6,4},{8,10},{10,8},{12,14},{14,12},{1,3},{3,1},... | collective-permute-start | bytes 442376 | tf_op jit(solution)/shard_map/ppermute | solution.py:396
  72.8 10.4 %collective-permute-start.11 = (bf16[144,512]{1,0:T(8,128)(2,1)S(1)}, bf16[144,512]{1,0:T(8,128)(2,1)S(1)}, u32[]{:S(2)}, u32[]{:S(2)}) collective-permute-start(bf16[144,512]{1,0:T(8,128)(2,1)S(1)} %collective-permute-done.10.refs_14_), channel_id=1, source_target_pairs={{0,2},{2,0},{4,6},{6,4},{8,10},{10,8},{12,14},{14,12},{1,3},{3,1},... | collective-permute-start | bytes 442376 | tf_op jit(solution)/shard_map/ppermute | solution.py:396
  73.9 10.9 %collective-permute-start.9 = (bf16[144,512]{1,0:T(8,128)(2,1)S(1)}, bf16[144,512]{1,0:T(8,128)(2,1)S(1)}, u32[]{:S(2)}, u32[]{:S(2)}) collective-permute-start(bf16[144,512]{1,0:T(8,128)(2,1)S(1)} %collective-permute-done.8.refs_12_), channel_id=1, source_target_pairs={{0,2},{2,0},{4,6},{6,4},{8,10},{10,8},{12,14},{14,12},{1,3},{3,1},... | collective-permute-start | bytes 442376 | tf_op jit(solution)/shard_map/ppermute | solution.py:396
  76.2 13.4 %collective-permute-start.19 = (bf16[32,1408]{1,0:T(8,128)(2,1)S(1)}, bf16[32,1408]{1,0:T(8,128)(2,1)S(1)}, u32[]{:S(2)}, u32[]{:S(2)}) collective-permute-start(bf16[32,1408]{1,0:T(8,128)(2,1)S(1)} %add_convert_fusion), channel_id=1, source_target_pairs={{0,2},{2,0},{4,6},{6,4},{8,10},{10,8},{12,14},{14,12},{1,3},{3,1},... | collective-permute-start | bytes 270344 | tf_op jit(solution)/shard_map/ppermute | solution.py:406
  77.5 7.3 %copy-start.4 = (bf16[144,512]{1,0:T(8,128)(2,1)}, bf16[144,512]{1,0:T(8,128)(2,1)S(1)}, u32[]{:S(2)}) copy-start(bf16[144,512]{1,0:T(8,128)(2,1)S(1)} %collective-permute-done.7.refs_11_) | copy-start | bytes 442372
  80.6 4.2 %copy-start.5 = (bf16[144,512]{1,0:T(8,128)(2,1)}, bf16[144,512]{1,0:T(8,128)(2,1)S(1)}, u32[]{:S(2)}) copy-start(bf16[144,512]{1,0:T(8,128)(2,1)S(1)} %collective-permute-done.13.refs_17_) | copy-start | bytes 442372
  89.7 12.7 %collective-permute-start.20 = (bf16[32,2816]{1,0:T(8,128)(2,1)S(1)}, bf16[32,2816]{1,0:T(8,128)(2,1)S(1)}, u32[]{:S(2)}, u32[]{:S(2)}) collective-permute-start(bf16[32,2816]{1,0:T(8,128)(2,1)S(1)} %pad_maximum_fusion), channel_id=1, source_target_pairs={{0,1},{1,0},{2,3},{3,2},{4,5},{5,4},{6,7},{7,6},{8,9},{9,8},{10,11... | collective-permute-start | bytes 540680 | tf_op jit(solution)/shard_map/ppermute | solution.py:422
  (8 other events, 12.7 us)
where the time goes:
time: 105 us; the launch traced here: 104 us
  starting transfers between devices  37.5 us (36%)
  Pallas kernels  34.4 us (33%)
  waiting for transfers between devices  26.4 us (25%)
  local copies, waits for them, and re-layouts  2.9 us (3%)
  other arithmetic  1.92 us (2%)
    ppermute x6, starting transfers between devices, gather_blocks(): lax.ppermute(block, 'node', [(i, i + d) for i in range(slots - d)])  21.2 us
    pallas_call x4, Pallas kernels, attend(): pl.pallas_call(functools.partial(attend_kernel, slots, LOG2E * inverse_ro...  16.9 us
    pallas_call x1, Pallas kernels, stats(): pl.pallas_call(functools.partial(stats_kernel, slots, scale), name='stats...  10.5 us
    ppermute x4, waiting for transfers between devices, swap(): return lax.ppermute(x, 'node', [(i, i ^ bit) for i in range(slots)])  10.3 us
    ppermute x8, starting transfers between devices, gather_blocks(): blocks += [column, lax.ppermute(column, 'node', swap)]  9.18 us
    ppermute x8, waiting for transfers between devices, gather_blocks(): blocks += [column, lax.ppermute(column, 'node', swap)]  7.67 us
    pallas_call x1, Pallas kernels, prepare(): pl.pallas_call(prepare_kernel, name='prepare', out_shape=(jax.ShapeDtypeS...  3.88 us
    all_to_all x1, starting transfers between devices, on_device(): received = lax.all_to_all(projected, 'node', 0, 0)  3.38 us
  transfers between devices with their start and end apart: 22, of which 12 were waited for; matrix products, arithmetic and copies ran while one was open for 0% of the time, Pallas kernels for 30%

commit v1 on v0

v1 whole, which is shorter than its diff:
```python
import functools

import jax
import jax.numpy as jnp
from jax import lax
from jax.experimental import pallas as pl
from jax.experimental.pallas import tpu as pltpu
from jax.sharding import PartitionSpec as P


HQ = 20
KEY_HEADS = 4
HEAD_SIZE = 128
PROMPT = 2
SPAN = 5
PER = HQ // KEY_HEADS

NEGATIVE = -1e30
LOG2E = 1.4426950408889634
F32 = jnp.float32
BF16 = jnp.bfloat16


VMEM_LIMIT = 56 * 1024 * 1024
SMALL_LIMIT = 16 * 1024 * 1024


def dot(a, b):
    return lax.dot_general(a, b, (((1,), (0,)), ((), ())), preferred_element_type=F32)


def dot_nt(a, b):
    return lax.dot_general(a, b, (((1,), (1,)), ((), ())), preferred_element_type=F32)


def dot_tn(a, b):
    return lax.dot_general(a, b, (((0,), (0,)), ((), ())), preferred_element_type=F32)


def paired(slots):
    return slots % 2 == 0 and slots <= 1 + PROMPT + SPAN


def candidate_count(slots):
    return slots if paired(slots) else 1 + PROMPT + SPAN


def candidate_slot(slots, own, c):
    if paired(slots):
        pair = own - (c // 2) * 2
        slot = pair + (c % 2) * (1 - 2 * (pair % 2))
        return jnp.where(pair >= 0, slot, -1)
    window = own - c
    window = jnp.where(window >= PROMPT, window, -1)
    prompt = c - SPAN - 1
    prompt = jnp.where(prompt < own, prompt, -1)
    return jnp.where(c == 0, own, jnp.where(c <= SPAN, window, prompt))


def value_index(slots, own, j):
    return jnp.maximum(own // 2 - j, 0) if paired(slots) else j


def mark_candidates(slots, parents_ref, lengths_ref, live_ref):
    own = lax.axis_index("node")
    count = candidate_count(slots)
    for c in range(count):
        live_ref[c] = 0
    live_ref[0] = lengths_ref[0, own]

    def climb(step, current):
        at = jnp.maximum(current, 0)
        for c in range(1, count):
            slot = candidate_slot(slots, own, c)

            @pl.when((slot == current) & (current >= 0))
            def _():
                live_ref[c] = lengths_ref[0, at]

        return jnp.where(current >= 0, parents_ref[0, at], -1)

    lax.fori_loop(0, PROMPT + SPAN, climb, parents_ref[0, own])


def prepare_kernel(
    lengths_ref, x_ref, down_ref, up_ref, frozen_ref, q_ref, g_ref,
    message_ref, low_ref, qt_ref, gt_ref,
):
    own = lax.axis_index("node")
    rows = x_ref.shape[0]
    low_t = dot_nt(down_ref[...], x_ref[...]).astype(BF16)
    values = frozen_ref[...].astype(F32) + dot_tn(low_t, up_ref[...])
    low_ref[...] = low_t
    for i in range(message_ref.shape[0]):
        message_ref[i] = values.astype(BF16)
    length = lengths_ref[0, own]
    live = lax.broadcasted_iota(jnp.int32, (rows, HEAD_SIZE), 0) < length
    for h in range(HQ):
        cols = slice(h * HEAD_SIZE, (h + 1) * HEAD_SIZE)
        here = slice(h * rows, (h + 1) * rows)
        qt_ref[:, here] = q_ref[:, cols].T
        g = jnp.where(live, g_ref[:, cols].astype(F32), 0.0).astype(BF16)
        gt_ref[:, here] = g.T


def prepare(copies, lengths, x, down_t, up, frozen, q, g):
    rows = x.shape[0]
    rank, width = up.shape
    vm = pl.BlockSpec(memory_space=pltpu.VMEM)
    return pl.pallas_call(
        prepare_kernel,
        name="prepare",
        out_shape=(
            jax.ShapeDtypeStruct((copies, rows, width), BF16),
            jax.ShapeDtypeStruct((rank, rows), BF16),
            jax.ShapeDtypeStruct((HEAD_SIZE, HQ * rows), BF16),
            jax.ShapeDtypeStruct((HEAD_SIZE, HQ * rows), BF16),
        ),
        in_specs=[pl.BlockSpec(memory_space=pltpu.SMEM)] + [vm] * 6,
        out_specs=(vm,) * 4,
        compiler_params=pltpu.CompilerParams(vmem_limit_bytes=VMEM_LIMIT),
        cost_estimate=pl.CostEstimate(flops=100_000_000, bytes_accessed=6_000_000, transcendentals=0),
    )(lengths, x, down_t, up, frozen, q, g)


def fill_masks(live_ref, mask_ref, causal_ref):
    rows = causal_ref.shape[0]
    key_at = lax.broadcasted_iota(jnp.int32, (rows, rows), 0)
    across = lax.broadcasted_iota(jnp.int32, (rows, rows), 1)
    for c in range(live_ref.shape[0]):
        dead = (across == 0) & (key_at >= live_ref[c])
        mask_ref[c * rows : (c + 1) * rows] = jnp.where(dead, NEGATIVE, 0.0).astype(BF16)
    causal_ref[...] = jnp.where(key_at <= across, 0.0, NEGATIVE)


def first_row(rows, lanes):
    return jnp.where(lax.broadcasted_iota(jnp.int32, (rows, lanes), 0) == 0, 1.0, 0.0).astype(BF16)


def fill_bias(live_ref, bias_ref):
    rows = bias_ref.shape[1]
    key_at = lax.broadcasted_iota(jnp.int32, (rows, rows), 0)
    query_at = lax.broadcasted_iota(jnp.int32, (rows, rows), 1)
    for c in range(live_ref.shape[0]):
        allowed = key_at < live_ref[c]
        if c == 0:
            allowed &= key_at <= query_at
        bias_ref[c] = jnp.where(allowed, 0.0, NEGATIVE)


def fold(x, op):
    return op(x.reshape(x.shape[0] // 8, 8, x.shape[1]), axis=0)


def stats_kernel(slots, scale, *refs):
    count = candidate_count(slots)
    parents_ref, lengths_ref = refs[:2]
    key_refs = refs[2 : 2 + count]
    qt_ref, gt_ref, up_ref, low_ref = refs[2 + count : 6 + count]
    proj_ref, part_ref, lse_ref = refs[6 + count : 9 + count]
    live_ref, keys, weights, bias, scores, shares, rest = refs[9 + count :]
    rows = key_refs[0].shape[0]
    own = lax.axis_index("node")
    mark_candidates(slots, parents_ref, lengths_ref, live_ref)
    fill_bias(live_ref, bias)
    for c in range(count):
        keys[c * rows : (c + 1) * rows] = key_refs[c][...]

    def lanes_of(h):
        return pl.ds(pl.multiple_of(h * rows, rows), rows)

    def step(it, carried):
        top, inverse = carried
        here = jnp.minimum(it, HQ - 1)
        before = jnp.clip(it - 1, 0, HQ - 1)
        last = jnp.maximum(it - 2, 0)
        columns = pl.ds(pl.multiple_of((here // PER) * HEAD_SIZE, HEAD_SIZE), HEAD_SIZE)
        q = qt_ref[:, lanes_of(here)]
        high = summed = None
        fresh = dot(keys[:, columns], q)
        for c in range(count):
            block = slice(c * rows, (c + 1) * rows)
            weights[block, lanes_of(last)] = (shares[block] * inverse).astype(BF16)
            p = jnp.exp2(scores[block] * scale - top)
            shares[block] = p
            part = fold(p, jnp.sum)
            summed = part if c == 0 else summed + part
            s = fresh[block] + bias[c]
            scores[block] = s
            most = fold(s, jnp.max)
            high = most if c == 0 else jnp.maximum(high, most)
        total = jnp.sum(summed, axis=0, keepdims=True)
        lse_ref[:, lanes_of(before)] = top + jnp.log2(total)
        return jnp.max(high, axis=0, keepdims=True) * scale, 1.0 / total

    empty = jnp.zeros((1, rows), F32)
    lax.fori_loop(0, HQ + 2, step, (empty, empty), unroll=2)
    for k in range(KEY_HEADS):
        lanes = slice(k * PER * rows, (k + 1) * PER * rows)
        cols = slice(k * HEAD_SIZE, (k + 1) * HEAD_SIZE)
        part = dot_nt(gt_ref[:, lanes], weights[:, lanes])
        high = part.astype(BF16)
        part_ref[cols] = high
        rest[cols] = (part - high.astype(F32)).astype(BF16)
    up = up_ref[...]
    proj = dot(up, part_ref[...]) + dot(up, rest[...])
    low = low_ref[...].astype(F32)
    for slot in range(slots):
        proj_ref[slot] = jnp.where(slot > own, low, 0.0)
    for c in range(count):

        @pl.when(live_ref[c] > 0)
        def _():
            proj_ref[candidate_slot(slots, own, c)] = proj[:, c * rows : (c + 1) * rows]


def stats(slots, parents, lengths, key_blocks, qt, gt, up, low):
    count = candidate_count(slots)
    rows, width = key_blocks[0].shape
    rank = up.shape[0]
    scale = LOG2E * HEAD_SIZE ** (-0.5)
    smem = pl.BlockSpec(memory_space=pltpu.SMEM)
    vm = pl.BlockSpec(memory_space=pltpu.VMEM)
    return pl.pallas_call(
        functools.partial(stats_kernel, slots, scale),
        name="stats",
        out_shape=(
            jax.ShapeDtypeStruct((slots, rank, rows), F32),
            jax.ShapeDtypeStruct((width, count * rows), BF16),
            jax.ShapeDtypeStruct((1, HQ * rows), F32),
        ),
        in_specs=[smem, smem] + [vm] * (count + 4),
        out_specs=(vm, vm, vm),
        scratch_shapes=[
            pltpu.SMEM((count,), jnp.int32),
            pltpu.VMEM((count * rows, width), BF16),
            pltpu.VMEM((count * rows, HQ * rows), BF16),
            pltpu.VMEM((count, rows, rows), F32),
            pltpu.VMEM((count * rows, rows), F32),
            pltpu.VMEM((count * rows, rows), F32),
            pltpu.VMEM((width, count * rows), BF16),
        ],
        compiler_params=pltpu.CompilerParams(vmem_limit_bytes=VMEM_LIMIT),
        cost_estimate=pl.CostEstimate(flops=2_000_000_000, bytes_accessed=5_000_000, transcendentals=3_000_000),
    )(parents, lengths, *key_blocks, qt, gt, up, low)


def attend_kernel(slots, group, scale, inverse_root, *refs):
    count = candidate_count(slots)
    parents_ref, lengths_ref = refs[:2]
    key_refs = refs[2 : 2 + count]
    value_refs = refs[2 + count : 4 + count]
    qt_ref, gt_ref, lse_ref = refs[4 + count : 7 + count]
    outs = refs[-13:-11]
    live_ref, keys, values, weights, rounded, slopes, masks, causal, out_t, done, sems = refs[-11:]
    rows = key_refs[0].shape[0]
    head = slice(group * HEAD_SIZE, (group + 1) * HEAD_SIZE)
    qt_ref, gt_ref, lse_ref = (
        ref.at[:, group * PER * rows : (group + 1) * PER * rows] for ref in (qt_ref, gt_ref, lse_ref)
    )
    own = lax.axis_index("node")
    mark_candidates(slots, parents_ref, lengths_ref, live_ref)
    fill_masks(live_ref, masks, causal)
    ones = first_row(HEAD_SIZE, rows)
    for c in range(count):
        block = slice(c * rows, (c + 1) * rows)
        keys[block] = key_refs[c][:, head]
        values[block] = value_refs[c % 2][value_index(slots, own, c // 2), :, head]
    for h in range(PER):
        here = slice(h * rows, (h + 1) * rows)
        s = dot(
            jnp.concatenate([keys[...], masks[...]], axis=1), jnp.concatenate([qt_ref[:, here], ones], axis=0)
        )
        for c in range(count):
            block = slice(c * rows, (c + 1) * rows)
            t = s[block] + causal[...] if c == 0 else s[block]
            w = jnp.exp2(t * scale - lse_ref[:, here])
            weights[block, here] = w
            rounded[block, here] = w.astype(BF16)
    values_t = values[...].T
    keys_t = keys[...].T
    out_t[...] = dot(values_t, rounded[...])
    dots = []
    for h in range(PER):
        here = slice(h * rows, (h + 1) * rows)
        dots.append(jnp.sum(gt_ref[:, here].astype(F32) * out_t[:, here], axis=0, keepdims=True))
    for h in range(PER):
        here = slice(h * rows, (h + 1) * rows)
        pressure = dot(values[...], gt_ref[:, here])
        slopes[:, here] = (weights[:, here] * (pressure - dots[h]) * inverse_root).astype(BF16)
    dq_t = dot(keys_t, slopes[...])
    live = lax.broadcasted_iota(jnp.int32, (rows, HEAD_SIZE), 0) < lengths_ref[0, own]
    for h in range(PER):
        cols = slice(h * HEAD_SIZE, (h + 1) * HEAD_SIZE)
        here = slice(h * rows, (h + 1) * rows)
        done[1, :, cols] = dq_t[:, here].T.astype(BF16)
        done[0, :, cols] = jnp.where(live, out_t[:, here].T, 0.0).astype(BF16)
    wide = PER * HEAD_SIZE
    copies = [
        pltpu.make_async_copy(done.at[i], out.at[:, group * wide : (group + 1) * wide], sems.at[i])
        for i, out in enumerate(outs)
    ]
    for copy in copies:
        copy.start()
    for copy in copies:
        copy.wait()


def attend(slots, group, carried, parents, lengths, key_blocks, value_pair, qt, gt, lse):
    count = candidate_count(slots)
    rows = key_blocks[0].shape[0]
    lanes = PER * rows
    inverse_root = HEAD_SIZE ** (-0.5)
    smem = pl.BlockSpec(memory_space=pltpu.SMEM)
    vm = pl.BlockSpec(memory_space=pltpu.VMEM)
    anywhere = pl.BlockSpec(memory_space=pl.ANY)
    first = 7 + count
    return pl.pallas_call(
        functools.partial(attend_kernel, slots, group, LOG2E * inverse_root, inverse_root),
        name="attend",
        out_shape=(jax.ShapeDtypeStruct((rows, HQ * HEAD_SIZE), BF16),) * 2,
        in_specs=[smem, smem] + [vm] * (count + 5) + [anywhere] * len(carried),
        out_specs=(anywhere, anywhere),
        scratch_shapes=[
            pltpu.SMEM((count,), jnp.int32),
            pltpu.VMEM((count * rows, HEAD_SIZE), BF16),
            pltpu.VMEM((count * rows, HEAD_SIZE), BF16),
            pltpu.VMEM((count * rows, lanes), F32),
            pltpu.VMEM((count * rows, lanes), BF16),
            pltpu.VMEM((count * rows, lanes), BF16),
            pltpu.VMEM((count * rows, rows), BF16),
            pltpu.VMEM((rows, rows), F32),
            pltpu.VMEM((HEAD_SIZE, lanes), F32),
            pltpu.VMEM((2, rows, PER * HEAD_SIZE), BF16),
            pltpu.SemaphoreType.DMA((2,)),
        ],
        input_output_aliases={first + i: i for i in range(len(carried))},
        compiler_params=pltpu.CompilerParams(vmem_limit_bytes=SMALL_LIMIT),
        cost_estimate=pl.CostEstimate(flops=800_000_000, bytes_accessed=1_500_000, transcendentals=700_000),
    )(parents, lengths, *key_blocks, *value_pair, qt, gt, lse, *carried)


def gradient_kernel(slots, factor, received_ref, x_ref, part_ref, low_ref, keep_ref, send_ref):
    rows, width = x_ref.shape
    core = lax.axis_index("rep")
    half = keep_ref.shape[1]
    start = width - half
    own = lax.axis_index("node")
    total = received_ref[own]
    for slot in range(slots):
        total += jnp.where(slot > own, received_ref[slot], 0.0)
    total = total.astype(BF16)

    def place(ref, which):
        if which == 0:
            ref[...] = dot(total, x_ref[:, :half]) * factor
        else:
            ref[:, :start] = dot(total, x_ref[:, half:]) * factor

    for mine in range(2):

        @pl.when(core == mine)
        def _():
            place(send_ref, 1 - mine)
            place(keep_ref, mine)

    low_t = [low_ref[...]]
    for c in range(1, part_ref.shape[1] // rows):
        low_t.append(received_ref[jnp.maximum(candidate_slot(slots, own, c), 0)].astype(BF16))
    up = dot_nt(jnp.concatenate(low_t, axis=1), part_ref[...]) * factor

    @pl.when(core == 0)
    def _():
        send_ref[:, start:] = up

    @pl.when(core == 1)
    def _():
        keep_ref[:, start:] = up


def gradients(slots, received, x, parts, low, factor):
    _, width = x.shape
    inner = parts.shape[0]
    rank = received.shape[1]
    half = (width + inner) // 2
    vm = pl.BlockSpec(memory_space=pltpu.VMEM)
    return pl.pallas_call(
        functools.partial(gradient_kernel, slots, factor),
        name="gradients",
        out_shape=(jax.ShapeDtypeStruct((rank, half), F32),) * 2,
        in_specs=[vm] * 4,
        out_specs=(vm, vm),
        compiler_params=pltpu.CompilerParams(vmem_limit_bytes=SMALL_LIMIT),
        cost_estimate=pl.CostEstimate(flops=80_000_000, bytes_accessed=4_000_000, transcendentals=0),
    )(received, x, parts, low)


def gather_keys(slots, block):
    if not paired(slots):
        return candidate_blocks(slots, block)
    columns = {0: block}
    for d in range(slots // 2 - 1, 0, -1):
        columns[d] = lax.ppermute(block, "node", [(i, i + 2 * d) for i in range(slots - 2 * d)])
    blocks = []
    for d in range(slots // 2):
        swap = [(i, i ^ 1) for i in range(2 * d, slots) if d or i % 2 == 0]
        blocks += [columns[d], lax.ppermute(columns[d], "node", swap)]
    return blocks


def candidate_blocks(slots, block):
    own = lax.axis_index("node")
    whole = lax.all_gather(block, "node")
    return [block] + [
        lax.dynamic_index_in_dim(whole, jnp.maximum(candidate_slot(slots, own, c), 0), 0, keepdims=False)
        for c in range(1, candidate_count(slots))
    ]


def gather_values(slots, message):
    if not paired(slots):
        blocks = candidate_blocks(slots, message[0])
        return jnp.stack(blocks[0::2]), jnp.stack(blocks[1::2])
    even = lax.all_to_all(
        message, "node", 0, 0, axis_index_groups=[list(range(y, slots, 2)) for y in range(2)]
    )
    odd = lax.ppermute(even, "node", [(i, i ^ 1) for i in range(slots)])
    return even, odd


def sum_over_all(slots, keep, send):
    core = lax.axis_index("rep")
    own = lax.axis_index("node")
    swap_core = [(0, 1), (1, 0)]

    def swap(x, bit):
        return lax.ppermute(x, "node", [(i, i ^ bit) for i in range(slots)])

    came = lax.ppermute(send, "rep", swap_core)
    total = keep + came
    quarter = total.shape[1] // 2
    low, high = total[:, :quarter], total[:, quarter:]
    odd = own % 2 == 1
    mine = jnp.where(odd, high, low)
    other = jnp.where(odd, low, high).astype(BF16)
    mine = (mine + swap(other, 1).astype(F32)).astype(BF16)
    bit = 2
    while bit < slots:
        mine = (mine.astype(F32) + swap(mine, bit).astype(F32)).astype(BF16)
        bit *= 2
    other = swap(mine, 1)
    half = jnp.concatenate([jnp.where(odd, other, mine), jnp.where(odd, mine, other)], axis=1)
    other = lax.ppermute(half, "rep", swap_core)
    second = core == 1
    whole = jnp.concatenate([jnp.where(second, other, half), jnp.where(second, half, other)], axis=1)
    return whole.astype(F32)


def on_device(
    normed_input,
    queries,
    rotated_key_heads,
    frozen_value_rows,
    adapter_down_weight,
    adapter_up_weight,
    output_gradient,
    parents,
    lengths,
):
    x = normed_input[0]
    rows, width = x.shape
    slots = lax.axis_size("node")
    key_blocks = gather_keys(slots, rotated_key_heads[0])
    message, low, qt, gt = prepare(
        slots // 2 if paired(slots) else 1,
        lengths,
        x,
        adapter_down_weight.T,
        adapter_up_weight,
        frozen_value_rows[0],
        queries[0],
        output_gradient[0],
    )
    value_pair = gather_values(slots, message)
    projected, parts, lse = stats(slots, parents, lengths, key_blocks, qt, gt, adapter_up_weight, low)
    received = lax.all_to_all(projected, "node", 0, 0)
    factor = (slots * lax.axis_size("rep") * rows) ** (-0.5)
    keep, send = gradients(slots, received, x, parts, low, factor)
    whole = sum_over_all(slots, keep, send)
    carried = ()
    for group in range(KEY_HEADS):
        carried = attend(slots, group, carried, parents, lengths, key_blocks, value_pair, qt, gt, lse)
    attended, query_grad = carried
    return (attended[None], query_grad[None], whole[:, :width].T, whole[:, width:])


def solution(mesh):
    tokens = P(("groups", "rep"), "node", None)
    trees = P(("groups", "rep"), None)
    return jax.shard_map(
        on_device,
        mesh=mesh,
        in_specs=(tokens,) * 4 + (P(), P()) + (tokens, trees, trees),
        out_specs=(tokens, tokens, P("groups", None), P("groups", None)),
        check_vma=False,
    )
```

time: 105 us -> 113 us (1.076)
  blocking collectives: 0 us -> 19.1 us
  starting transfers between devices: 37.5 us -> 24.4 us
  waiting for transfers between devices: 26.4 us -> 34.8 us
  Pallas kernels: 34.4 us -> 28.9 us
    all_to_all x0 -> x1, blocking collectives: none -> 19.1 us  [on_device(): received = lax.all_to_all(projected, 'node', 0, 0)]
    ppermute x15 -> x8, starting transfers between devices: 32.3 us -> 17.2 us  [the longest x3 10.8 us: gather_keys(): lax.ppermute(block, 'node', [(i, i + 2 * d) for i in range(slots - 2 * d)])]
    ppermute x4, waiting for transfers between devices: 10.3 us -> 23.8 us  [swap(): return lax.ppermute(x, 'node', [(i, i ^ bit) for i in range(slots)])]
    pallas_call x5, Pallas kernels: 20.1 us -> 14.6 us  [the longest x4 13.9 us: attend(): pl.pallas_call(functools.partial(attend_kernel, slots, group, LOG2E * inv...]
    all_to_all x1, waiting for transfers between devices: 2.74 us -> 0.01 us  [gather_values(): lax.all_to_all(message, 'node', 0, 0, axis_index_groups=[list(range(y, sl...]
    ppermute x15 -> x8, waiting for transfers between devices: 11.4 us -> 9.35 us  [the longest x1 9.25 us: gather_values(): odd = lax.ppermute(even, 'node', [(i, i ^ 1) for i in range(slots)])]
    ppermute x4, starting transfers between devices: 1.72 us -> 3.34 us  [swap(): return lax.ppermute(x, 'node', [(i, i ^ bit) for i in range(slots)])]
  transfers between devices with their start and end apart: 22 -> 15, of which waited for: 12 -> 7; matrix products, arithmetic and copies ran while one was open for 0% -> 0% of each run, Pallas kernels for 30% -> 16%
where the time goes in v1:
time: 113 us; the launch traced here: 112 us
  waiting for transfers between devices  34.8 us (31%)
  Pallas kernels  28.9 us (26%)
  starting transfers between devices  24.4 us (22%)
  blocking collectives  19.1 us (17%)
  local copies, waits for them, and re-layouts  2.93 us (3%)
    ppermute x4, waiting for transfers between devices, swap(): return lax.ppermute(x, 'node', [(i, i ^ bit) for i in range(slots)])  23.8 us
    all_to_all x1, blocking collectives, on_device(): received = lax.all_to_all(projected, 'node', 0, 0)  19.1 us
    pallas_call x4, Pallas kernels, attend(): pl.pallas_call(functools.partial(attend_kernel, slots, group, LOG2E * inv...  13.9 us
    ppermute x3, starting transfers between devices, gather_keys(): lax.ppermute(block, 'node', [(i, i + 2 * d) for i in range(slots - 2 * d)])  10.8 us
    pallas_call x1, Pallas kernels, stats(): pl.pallas_call(functools.partial(stats_kernel, slots, scale), name='stats...  10.4 us
    ppermute x1, waiting for transfers between devices, gather_values(): odd = lax.ppermute(even, 'node', [(i, i ^ 1) for i in range(slots)])  9.25 us
    ppermute x4, starting transfers between devices, gather_keys(): blocks += [columns[d], lax.ppermute(columns[d], 'node', swap)]  5.43 us
    pallas_call x1, Pallas kernels, prepare(): pl.pallas_call(prepare_kernel, name='prepare', out_shape=(jax.ShapeDtypeS...  3.85 us
  transfers between devices with their start and end apart: 15, of which 7 were waited for; matrix products, arithmetic and copies ran while one was open for 0% of the time, Pallas kernels for 16%

profile of v1, /device:TPU:0, one launch (start us, length us, event | category | flops | bytes accessed | tf_op | source)
XLA Modules:
  0.0 112.2 jit_solution(14791285551716681551)
XLA Ops:
  0.6 7.0 %collective-permute-start.5 = (bf16[128,512]{1,0:T(8,128)(2,1)}, bf16[128,512]{1,0:T(8,128)(2,1)S(1)}, u32[]{:S(2)}, u32[]{:S(2)}) collective-permute-start(bf16[128,512]{1,0:T(8,128)(2,1)} %bitcast.12), channel_id=1, source_target_pairs={{0,12},{2,14},{1,13},{3,15},{16,28},{18,30},{17,29},{19,31}} | collective-permute-start | bytes 393224 | tf_op jit(solution)/shard_map/ppermute | solution.py:403
  7.6 1.3 %collective-permute-start.3 = (bf16[128,512]{1,0:T(8,128)(2,1)}, bf16[128,512]{1,0:T(8,128)(2,1)S(1)}, u32[]{:S(2)}, u32[]{:S(2)}) collective-permute-start(bf16[128,512]{1,0:T(8,128)(2,1)} %bitcast.13), channel_id=1, source_target_pairs={{0,8},{2,10},{4,12},{6,14},{1,9},{3,11},{5,13},{7,15},{16,24},{18,... | collective-permute-start | bytes 393224 | tf_op jit(solution)/shard_map/ppermute | solution.py:403
  8.9 2.5 %collective-permute-start.1 = (bf16[128,512]{1,0:T(8,128)(2,1)}, bf16[128,512]{1,0:T(8,128)(2,1)S(1)}, u32[]{:S(2)}, u32[]{:S(2)}) collective-permute-start(bf16[128,512]{1,0:T(8,128)(2,1)} %bitcast.14), channel_id=1, source_target_pairs={{0,4},{2,6},{4,8},{6,10},{8,12},{10,14},{1,5},{3,7},{5,9},{7,11},{... | collective-permute-start | bytes 393224 | tf_op jit(solution)/shard_map/ppermute | solution.py:403
  11.4 3.4 %collective-permute-start = (bf16[128,512]{1,0:T(8,128)(2,1)}, bf16[128,512]{1,0:T(8,128)(2,1)S(1)}, u32[]{:S(2)}, u32[]{:S(2)}) collective-permute-start(bf16[128,512]{1,0:T(8,128)(2,1)} %bitcast.15), channel_id=1, source_target_pairs={{0,2},{4,6},{8,10},{12,14},{1,3},{5,7},{9,11},{13,15},{16,18},{20,... | collective-permute-start | bytes 393224 | tf_op jit(solution)/shard_map/ppermute | solution.py:407
  14.9 0.7 collective-permute-start.6
  15.6 0.7 collective-permute-start.4
  16.3 0.1 collective-permute-done.1.refs_4_
  16.3 0.7 collective-permute-start.2
  17.0 3.8 %prepare.1 = (bf16[4,128,512]{2,1,0:T(8,128)(2,1)}, bf16[32,128]{1,0:T(8,128)(2,1)}, bf16[128,2560]{1,0:T(8,128)(2,1)}, bf16[128,2560]{1,0:T(8,128)(2,1)}) custom-call(s32[1,8]{1,0:T(1,128)} %refs_1_.9, bf16[128,5120]{1,0:T(8,128)(2,1)} %bitcast.10, bf16[32,5120]{1,0:T(8,128)(2,1)} %bitcast.25, bf16[32,512]{1,0:T(8,128)(2,1)} %refs_12_.1, ...), custom_call_target="tpu_custom_call" | custom-call | flops 100000000 | bytes 6000000 | tf_op jit(solution)/shard_map/prepare/pallas_call | solution.py:110
  21.0 0.6 copy-done.10
  21.7 10.4 %stats.1 = (f32[8,32,128]{2,1,0:T(8,128)}, bf16[512,1024]{1,0:T(8,128)(2,1)}, f32[1,2560]{1,0:T(1,128)}) custom-call(s32[1,8]{1,0:T(1,128)} %refs_0_.9, s32[1,8]{1,0:T(1,128)} %refs_1_.9, bf16[128,512]{1,0:T(8,128)(2,1)} %bitcast.16, bf16[128,512]{1,0:T(8,128)(2,1)} %copy-done.10, bf16[128,512]{1,0:T(8,128)(2,1)} %copy-done.8, bf16[128,512]{1,0:T(8,128)(2,1)} %copy-done.16, ...), custom_call_target="tpu_custom_call" | custom-call | flops 2000000000 | bytes 5000000 | tf_op jit(solution)/shard_map/stats/pallas_call | solution.py:224
  32.1 19.1 %all_to_all.10.received_ref = f32[8,32,128]{2,1,0:T(8,128)S(1)} all-to-all(f32[8,32,128]{2,1,0:T(8,128)} %get-tuple-element.34), channel_id=1, replica_groups=mesh['groups'=2,'node'=8,'rep'=2] {'node'}, dimensions={0} | all-to-all | bytes 262144 | tf_op jit(solution)/shard_map/all_to_all | solution.py:486
  51.2 1.2 %copy-done.18 = bf16[512,1024]{1,0:T(8,128)(2,1)S(1)} copy-done((bf16[512,1024]{1,0:T(8,128)(2,1)S(1)}, bf16[512,1024]{1,0:T(8,128)(2,1)}, u32[]{:S(2)}) %copy-start.18) | copy-done | bytes 1048600
  52.5 0.7 gradients.1
  53.3 1.6 %collective-permute-done.8 = f32[32,2816]{1,0:T(8,128)S(1)} collective-permute-done((f32[32,2816]{1,0:T(8,128)S(1)}, f32[32,2816]{1,0:T(8,128)S(1)}, u32[]{:S(2)}, u32[]{:S(2)}) %collective-permute-start.8) | collective-permute-done | bytes 360480 | tf_op jit(solution)/shard_map/ppermute | solution.py:439
  55.1 0.3 collective-permute-start.9
  55.4 4.4 %collective-permute-done.9 = bf16[32,1408]{1,0:T(8,128)(2,1)S(1)} collective-permute-done((bf16[32,1408]{1,0:T(8,128)(2,1)S(1)}, bf16[32,1408]{1,0:T(8,128)(2,1)S(1)}, u32[]{:S(2)}, u32[]{:S(2)}) %collective-permute-start.9) | collective-permute-done | bytes 90144 | tf_op jit(solution)/shard_map/ppermute | solution.py:437
  59.9 0.1 collective-permute-start.10
  60.0 3.7 %all-to-all-start = ((bf16[4,128,512]{2,1,0:T(8,128)(2,1)}), bf16[4,128,512]{2,1,0:T(8,128)(2,1)S(1)}, u32[]{:S(2)}, u32[]{:S(2)}) async-start(bf16[4,128,512]{2,1,0:T(8,128)(2,1)} %get-tuple-element.21), calls=%async_computation | async-start | bytes 1048576 | tf_op jit(solution)/shard_map/all_to_all | solution.py:424
  63.7 0.8 collective-permute-done.10
  64.5 1.9 %collective-permute-start.11 = (bf16[32,1408]{1,0:T(8,128)(2,1)S(1)}, bf16[32,1408]{1,0:T(8,128)(2,1)S(1)}, u32[]{:S(2)}, u32[]{:S(2)}) collective-permute-start(bf16[32,1408]{1,0:T(8,128)(2,1)S(1)} %add_convert_fusion.1), channel_id=1, source_target_pairs={{0,8},{2,10},{4,12},{6,14},{8,0},{10,2},{12,4},{14,6},{1,9},{3,11}... | collective-permute-start | bytes 270344 | tf_op jit(solution)/shard_map/ppermute | solution.py:437
  66.5 15.1 %collective-permute-done.11 = bf16[32,1408]{1,0:T(8,128)(2,1)S(1)} collective-permute-done((bf16[32,1408]{1,0:T(8,128)(2,1)S(1)}, bf16[32,1408]{1,0:T(8,128)(2,1)S(1)}, u32[]{:S(2)}, u32[]{:S(2)}) %collective-permute-start.11) | collective-permute-done | bytes 90144 | tf_op jit(solution)/shard_map/ppermute | solution.py:437
  81.5 1.1 collective-permute-start.12
  82.6 1.0 collective-permute-start.7
  83.6 3.5 %collective-permute-done.12 = bf16[32,1408]{1,0:T(8,128)(2,1)S(1)} collective-permute-done((bf16[32,1408]{1,0:T(8,128)(2,1)S(1)}, bf16[32,1408]{1,0:T(8,128)(2,1)S(1)}, u32[]{:S(2)}, u32[]{:S(2)}) %collective-permute-start.12) | collective-permute-done | bytes 90144 | tf_op jit(solution)/shard_map/ppermute | solution.py:437
  87.2 9.3 %collective-permute-done.7.refs_11_ = bf16[4,128,512]{2,1,0:T(8,128)(2,1)S(1)} collective-permute-done((bf16[4,128,512]{2,1,0:T(8,128)(2,1)S(1)}, bf16[4,128,512]{2,1,0:T(8,128)(2,1)S(1)}, u32[]{:S(2)}, u32[]{:S(2)}) %collective-permute-start.7) | collective-permute-done | bytes 524320 | tf_op jit(solution)/shard_map/ppermute | solution.py:427
  96.6 3.5 %attend.4 = (bf16[128,2560]{1,0:T(8,128)(2,1)}, bf16[128,2560]{1,0:T(8,128)(2,1)}) custom-call(s32[1,8]{1,0:T(1,128)S(1)} %copy-done.22, s32[1,8]{1,0:T(1,128)S(1)} %copy-done.20, bf16[128,512]{1,0:T(8,128)(2,1)S(1)} %bitcast.17, bf16[128,512]{1,0:T(8,128)(2,1)S(1)} %copy-done.11, bf16[128,512]{1,0:T(8,128)(2,1)S(1)} %copy-done.9, ...), custom_call_target="tpu_custom_call" | custom-call | flops 800000000 | bytes 1500000 | tf_op jit(solution)/shard_map/attend/pallas_call | solution.py:318
  100.1 3.5 %attend.5 = (bf16[128,2560]{1,0:T(8,128)(2,1)}, bf16[128,2560]{1,0:T(8,128)(2,1)}) custom-call(s32[1,8]{1,0:T(1,128)S(1)} %copy-done.22, s32[1,8]{1,0:T(1,128)S(1)} %copy-done.20, bf16[128,512]{1,0:T(8,128)(2,1)S(1)} %bitcast.18, bf16[128,512]{1,0:T(8,128)(2,1)S(1)} %copy-done.11, ...), custom_call_target="tpu_custom_call", output_to_operand_aliasing={{0}: (15, {}), {1}: (16, {})} | custom-call | flops 800000000 | bytes 1500000 | tf_op jit(solution)/shard_map/attend/pallas_call | solution.py:318
  103.5 3.5 %attend.6 = (bf16[128,2560]{1,0:T(8,128)(2,1)}, bf16[128,2560]{1,0:T(8,128)(2,1)}) custom-call(s32[1,8]{1,0:T(1,128)S(1)} %copy-done.22, s32[1,8]{1,0:T(1,128)S(1)} %copy-done.20, bf16[128,512]{1,0:T(8,128)(2,1)S(1)} %bitcast.19, bf16[128,512]{1,0:T(8,128)(2,1)S(1)} %copy-done.11, ...), custom_call_target="tpu_custom_call", output_to_operand_aliasing={{0}: (15, {}), {1}: (16, {})} | custom-call | flops 800000000 | bytes 1500000 | tf_op jit(solution)/shard_map/attend/pallas_call | solution.py:318
  107.0 3.5 %attend.7 = (bf16[128,2560]{1,0:T(8,128)(2,1)}, bf16[128,2560]{1,0:T(8,128)(2,1)}) custom-call(s32[1,8]{1,0:T(1,128)S(1)} %copy-done.22, s32[1,8]{1,0:T(1,128)S(1)} %copy-done.20, bf16[128,512]{1,0:T(8,128)(2,1)S(1)} %bitcast.20, bf16[128,512]{1,0:T(8,128)(2,1)S(1)} %copy-done.11, ...), custom_call_target="tpu_custom_call", output_to_operand_aliasing={{0}: (15, {}), {1}: (16, {})} | custom-call | flops 800000000 | bytes 1500000 | tf_op jit(solution)/shard_map/attend/pallas_call | solution.py:318
  110.6 0.6 maximum_convert_fusion.1
  111.3 0.9 slice_bitcast_fusion
  (63 shorter events, 0.7 us)
Async XLA Ops:
  0.6 14.2 %collective-permute-start.5 = (bf16[128,512]{1,0:T(8,128)(2,1)}, bf16[128,512]{1,0:T(8,128)(2,1)S(1)}, u32[]{:S(2)}, u32[]{:S(2)}) collective-permute-start(bf16[128,512]{1,0:T(8,128)(2,1)} %bitcast.12), channel_id=1, source_target_pairs={{0,12},{2,14},{1,13},{3,15},{16,28},{18,30},{17,29},{19,31}} | collective-permute-start | bytes 393224 | tf_op jit(solution)/shard_map/ppermute | solution.py:403
  7.6 7.9 %collective-permute-start.3 = (bf16[128,512]{1,0:T(8,128)(2,1)}, bf16[128,512]{1,0:T(8,128)(2,1)S(1)}, u32[]{:S(2)}, u32[]{:S(2)}) collective-permute-start(bf16[128,512]{1,0:T(8,128)(2,1)} %bitcast.13), channel_id=1, source_target_pairs={{0,8},{2,10},{4,12},{6,14},{1,9},{3,11},{5,13},{7,15},{16,24},{18,... | collective-permute-start | bytes 393224 | tf_op jit(solution)/shard_map/ppermute | solution.py:403
  8.9 7.4 %collective-permute-start.1 = (bf16[128,512]{1,0:T(8,128)(2,1)}, bf16[128,512]{1,0:T(8,128)(2,1)S(1)}, u32[]{:S(2)}, u32[]{:S(2)}) collective-permute-start(bf16[128,512]{1,0:T(8,128)(2,1)} %bitcast.14), channel_id=1, source_target_pairs={{0,4},{2,6},{4,8},{6,10},{8,12},{10,14},{1,5},{3,7},{5,9},{7,11},{... | collective-permute-start | bytes 393224 | tf_op jit(solution)/shard_map/ppermute | solution.py:403
  11.4 9.5 %collective-permute-start = (bf16[128,512]{1,0:T(8,128)(2,1)}, bf16[128,512]{1,0:T(8,128)(2,1)S(1)}, u32[]{:S(2)}, u32[]{:S(2)}) collective-permute-start(bf16[128,512]{1,0:T(8,128)(2,1)} %bitcast.15), channel_id=1, source_target_pairs={{0,2},{4,6},{8,10},{12,14},{1,3},{5,7},{9,11},{13,15},{16,18},{20,... | collective-permute-start | bytes 393224 | tf_op jit(solution)/shard_map/ppermute | solution.py:407
  14.9 6.0 %copy-start.4 = (bf16[128,512]{1,0:T(8,128)(2,1)}, bf16[128,512]{1,0:T(8,128)(2,1)S(1)}, u32[]{:S(2)}) copy-start(bf16[128,512]{1,0:T(8,128)(2,1)S(1)} %collective-permute-done.5.refs_8_) | copy-start | bytes 393220
  14.9 6.0 %collective-permute-start.6 = (bf16[128,512]{1,0:T(8,128)(2,1)S(1)}, bf16[128,512]{1,0:T(8,128)(2,1)S(1)}, u32[]{:S(2)}, u32[]{:S(2)}) collective-permute-start(bf16[128,512]{1,0:T(8,128)(2,1)S(1)} %collective-permute-done.5.refs_8_), channel_id=1, source_target_pairs={{12,14},{14,12},{13,15},{15,13},{28,30},{30,28},{29,31},{31,29}} | collective-permute-start | bytes 393224 | tf_op jit(solution)/shard_map/ppermute | solution.py:407
  15.6 5.3 %copy-start.6 = (bf16[128,512]{1,0:T(8,128)(2,1)}, bf16[128,512]{1,0:T(8,128)(2,1)S(1)}, u32[]{:S(2)}) copy-start(bf16[128,512]{1,0:T(8,128)(2,1)S(1)} %collective-permute-done.3.refs_6_) | copy-start | bytes 393220
  15.6 5.3 %collective-permute-start.4 = (bf16[128,512]{1,0:T(8,128)(2,1)S(1)}, bf16[128,512]{1,0:T(8,128)(2,1)S(1)}, u32[]{:S(2)}, u32[]{:S(2)}) collective-permute-start(bf16[128,512]{1,0:T(8,128)(2,1)S(1)} %collective-permute-done.3.refs_6_), channel_id=1, source_target_pairs={{8,10},{10,8},{12,14},{14,12},{9,11},{11,9},{13,15},{15,13},{24,26... | collective-permute-start | bytes 393224 | tf_op jit(solution)/shard_map/ppermute | solution.py:407
  16.3 4.6 %collective-permute-start.2 = (bf16[128,512]{1,0:T(8,128)(2,1)S(1)}, bf16[128,512]{1,0:T(8,128)(2,1)S(1)}, u32[]{:S(2)}, u32[]{:S(2)}) collective-permute-start(bf16[128,512]{1,0:T(8,128)(2,1)S(1)} %collective-permute-done.1.refs_4_), channel_id=1, source_target_pairs={{4,6},{6,4},{8,10},{10,8},{12,14},{14,12},{5,7},{7,5},{9,11},{11,9... | collective-permute-start | bytes 393224 | tf_op jit(solution)/shard_map/ppermute | solution.py:407
  21.7 29.5 %copy-start.2 = (bf16[1,128,5120]{2,1,0:T(8,128)(2,1)S(1)}, bf16[1,128,5120]{2,1,0:T(8,128)(2,1)}, u32[]{:S(2)}) copy-start(bf16[1,128,5120]{2,1,0:T(8,128)(2,1)} %param.9) | copy-start | bytes 3932164
  21.7 29.5 %copy-start.21 = (bf16[32,128]{1,0:T(8,128)(2,1)S(1)}, bf16[32,128]{1,0:T(8,128)(2,1)}, u32[]{:S(2)}) copy-start(bf16[32,128]{1,0:T(8,128)(2,1)} %get-tuple-element.24.refs_13_.low_ref) | copy-start | bytes 24580
  53.2 1.7 %collective-permute-start.8 = (f32[32,2816]{1,0:T(8,128)S(1)}, f32[32,2816]{1,0:T(8,128)S(1)}, u32[]{:S(2)}, u32[]{:S(2)}) collective-permute-start(f32[32,2816]{1,0:T(8,128)S(1)} %get-tuple-element.37), channel_id=1, source_target_pairs={{0,1},{1,0},{2,3},{3,2},{4,5},{5,4},{6,7},{7,6},{8,9},{9,8},{10,11... | collective-permute-start | bytes 1081352 | tf_op jit(solution)/shard_map/ppermute | solution.py:439
  55.0 41.5 %copy-start = (bf16[128,2560]{1,0:T(8,128)(2,1)S(1)}, bf16[128,2560]{1,0:T(8,128)(2,1)}, u32[]{:S(2)}) copy-start(bf16[128,2560]{1,0:T(8,128)(2,1)} %get-tuple-element.22.refs_10_.refs_12_) | copy-start | bytes 1966084
  55.0 41.5 %copy-start.1 = (bf16[128,2560]{1,0:T(8,128)(2,1)S(1)}, bf16[128,2560]{1,0:T(8,128)(2,1)}, u32[]{:S(2)}) copy-start(bf16[128,2560]{1,0:T(8,128)(2,1)} %get-tuple-element.23.refs_11_.refs_13_) | copy-start | bytes 1966084
  55.0 41.5 %copy-start.3 = (bf16[1,128,512]{2,1,0:T(8,128)(2,1)S(1)}, bf16[1,128,512]{2,1,0:T(8,128)(2,1)}, u32[]{:S(2)}) copy-start(bf16[1,128,512]{2,1,0:T(8,128)(2,1)} %param.11) | copy-start | bytes 393220
  55.0 41.5 %copy-start.5 = (bf16[128,512]{1,0:T(8,128)(2,1)S(1)}, bf16[128,512]{1,0:T(8,128)(2,1)}, u32[]{:S(2)}) copy-start(bf16[128,512]{1,0:T(8,128)(2,1)} %copy-done.4) | copy-start | bytes 393220
  55.0 41.5 %copy-start.7 = (bf16[128,512]{1,0:T(8,128)(2,1)S(1)}, bf16[128,512]{1,0:T(8,128)(2,1)}, u32[]{:S(2)}) copy-start(bf16[128,512]{1,0:T(8,128)(2,1)} %copy-done.6) | copy-start | bytes 393220
  55.1 41.5 %copy-start.9 = (bf16[128,512]{1,0:T(8,128)(2,1)S(1)}, bf16[128,512]{1,0:T(8,128)(2,1)}, u32[]{:S(2)}) copy-start(bf16[128,512]{1,0:T(8,128)(2,1)} %copy-done.8) | copy-start | bytes 393220
  55.1 41.5 %copy-start.11 = (bf16[128,512]{1,0:T(8,128)(2,1)S(1)}, bf16[128,512]{1,0:T(8,128)(2,1)}, u32[]{:S(2)}) copy-start(bf16[128,512]{1,0:T(8,128)(2,1)} %copy-done.10) | copy-start | bytes 393220
  55.1 41.5 %copy-start.13 = (bf16[128,512]{1,0:T(8,128)(2,1)S(1)}, bf16[128,512]{1,0:T(8,128)(2,1)}, u32[]{:S(2)}) copy-start(bf16[128,512]{1,0:T(8,128)(2,1)} %copy-done.12) | copy-start | bytes 393220
  55.1 41.5 %copy-start.15 = (bf16[128,512]{1,0:T(8,128)(2,1)S(1)}, bf16[128,512]{1,0:T(8,128)(2,1)}, u32[]{:S(2)}) copy-start(bf16[128,512]{1,0:T(8,128)(2,1)} %copy-done.14) | copy-start | bytes 393220
  55.1 41.5 %copy-start.17 = (bf16[128,512]{1,0:T(8,128)(2,1)S(1)}, bf16[128,512]{1,0:T(8,128)(2,1)}, u32[]{:S(2)}) copy-start(bf16[128,512]{1,0:T(8,128)(2,1)} %copy-done.16) | copy-start | bytes 393220
  55.1 41.5 %copy-start.19 = (f32[1,2560]{1,0:T(1,128)S(1)}, f32[1,2560]{1,0:T(1,128)}, u32[]{:S(2)}) copy-start(f32[1,2560]{1,0:T(1,128)} %get-tuple-element.25.refs_14_) | copy-start | bytes 30724
  55.1 41.5 %copy-start.20 = (s32[1,8]{1,0:T(1,128)S(1)}, s32[1,8]{1,0:T(1,128)}, u32[]{:S(2)}) copy-start(s32[1,8]{1,0:T(1,128)} %refs_1_.9) | copy-start | bytes 100
  55.1 41.4 %copy-start.22 = (s32[1,8]{1,0:T(1,128)S(1)}, s32[1,8]{1,0:T(1,128)}, u32[]{:S(2)}) copy-start(s32[1,8]{1,0:T(1,128)} %refs_0_.9) | copy-start | bytes 100
  55.1 4.7 %collective-permute-start.9 = (bf16[32,1408]{1,0:T(8,128)(2,1)S(1)}, bf16[32,1408]{1,0:T(8,128)(2,1)S(1)}, u32[]{:S(2)}, u32[]{:S(2)}) collective-permute-start(bf16[32,1408]{1,0:T(8,128)(2,1)S(1)} %select_convert_fusion), channel_id=1, source_target_pairs={{0,2},{2,0},{4,6},{6,4},{8,10},{10,8},{12,14},{14,12},{1,3},{3,1},... | collective-permute-start | bytes 270344 | tf_op jit(solution)/shard_map/ppermute | solution.py:437
  59.9 4.6 %collective-permute-start.10 = (bf16[32,1408]{1,0:T(8,128)(2,1)S(1)}, bf16[32,1408]{1,0:T(8,128)(2,1)S(1)}, u32[]{:S(2)}, u32[]{:S(2)}) collective-permute-start(bf16[32,1408]{1,0:T(8,128)(2,1)S(1)} %add_convert_fusion.2), channel_id=1, source_target_pairs={{0,4},{2,6},{4,0},{6,2},{8,12},{10,14},{12,8},{14,10},{1,5},{3,7},... | collective-permute-start | bytes 270344 | tf_op jit(solution)/shard_map/ppermute | solution.py:437
  60.0 22.6 %all-to-all-start = ((bf16[4,128,512]{2,1,0:T(8,128)(2,1)}), bf16[4,128,512]{2,1,0:T(8,128)(2,1)S(1)}, u32[]{:S(2)}, u32[]{:S(2)}) async-start(bf16[4,128,512]{2,1,0:T(8,128)(2,1)} %get-tuple-element.21), calls=%async_computation | async-start | bytes 1048576 | tf_op jit(solution)/shard_map/all_to_all | solution.py:424
  64.5 17.0 %collective-permute-start.11 = (bf16[32,1408]{1,0:T(8,128)(2,1)S(1)}, bf16[32,1408]{1,0:T(8,128)(2,1)S(1)}, u32[]{:S(2)}, u32[]{:S(2)}) collective-permute-start(bf16[32,1408]{1,0:T(8,128)(2,1)S(1)} %add_convert_fusion.1), channel_id=1, source_target_pairs={{0,8},{2,10},{4,12},{6,14},{8,0},{10,2},{12,4},{14,6},{1,9},{3,11}... | collective-permute-start | bytes 270344 | tf_op jit(solution)/shard_map/ppermute | solution.py:437
  81.5 5.6 %collective-permute-start.12 = (bf16[32,1408]{1,0:T(8,128)(2,1)S(1)}, bf16[32,1408]{1,0:T(8,128)(2,1)S(1)}, u32[]{:S(2)}, u32[]{:S(2)}) collective-permute-start(bf16[32,1408]{1,0:T(8,128)(2,1)S(1)} %add_convert_fusion), channel_id=1, source_target_pairs={{0,2},{2,0},{4,6},{6,4},{8,10},{10,8},{12,14},{14,12},{1,3},{3,1},... | collective-permute-start | bytes 270344 | tf_op jit(solution)/shard_map/ppermute | solution.py:437
  82.6 13.9 %collective-permute-start.7 = (bf16[4,128,512]{2,1,0:T(8,128)(2,1)S(1)}, bf16[4,128,512]{2,1,0:T(8,128)(2,1)S(1)}, u32[]{:S(2)}, u32[]{:S(2)}) collective-permute-start(bf16[4,128,512]{2,1,0:T(8,128)(2,1)S(1)} %all-to-all-done.refs_10_), channel_id=1, source_target_pairs={{0,2},{2,0},{4,6},{6,4},{8,10},{10,8},{12,14},{14,12},{1,3},{3,1},... | collective-permute-start | bytes 1572872 | tf_op jit(solution)/shard_map/ppermute | solution.py:427
  87.1 23.4 %collective-permute-start.13 = (bf16[32,2816]{1,0:T(8,128)(2,1)S(1)}, bf16[32,2816]{1,0:T(8,128)(2,1)S(1)}, u32[]{:S(2)}, u32[]{:S(2)}) collective-permute-start(bf16[32,2816]{1,0:T(8,128)(2,1)S(1)} %pad_maximum_fusion), channel_id=1, source_target_pairs={{0,1},{1,0},{2,3},{3,2},{4,5},{5,4},{6,7},{7,6},{8,9},{9,8},{10,11... | collective-permute-start | bytes 540680 | tf_op jit(solution)/shard_map/ppermute | solution.py:453
  (6 other events, 8.6 us)

commit v2 on v1

--- a/solution.py
+++ b/solution.py
@@ -80,6 +80,13 @@
         return jnp.where(current >= 0, parents_ref[0, at], -1)
 
     lax.fori_loop(0, PROMPT + SPAN, climb, parents_ref[0, own])
+
+
+def copies_of(pairs, sems, first=0):
+    copies = [pltpu.make_async_copy(source, target, sems.at[first + i]) for i, (source, target) in enumerate(pairs)]
+    for copy in copies:
+        copy.start()
+    return copies
 
 
 def prepare_kernel(
@@ -340,42 +347,40 @@
     )(parents, lengths, *key_blocks, *value_pair, qt, gt, lse, *carried)
 
 
-def gradient_kernel(slots, factor, received_ref, x_ref, part_ref, low_ref, keep_ref, send_ref):
-    rows, width = x_ref.shape
+def gradient_kernel(slots, factor, received_hbm, x_ref, part_ref, low_ref, keep_hbm, send_hbm, received_ref, halves, sems):
+    width = x_ref.shape[1]
     core = lax.axis_index("rep")
-    half = keep_ref.shape[1]
+    own = lax.axis_index("node")
+    half = halves.shape[2]
     start = width - half
-    own = lax.axis_index("node")
+    (arrival,) = copies_of([(received_hbm, received_ref)], sems)
+    arrival.wait()
     total = received_ref[own]
     for slot in range(slots):
         total += jnp.where(slot > own, received_ref[slot], 0.0)
     total = total.astype(BF16)
-
-    def place(ref, which):
+    low_t = [low_ref[...]]
+    for c in range(1, part_ref.shape[1] // low_ref.shape[1]):
+        low_t.append(received_ref[jnp.maximum(candidate_slot(slots, own, c), 0)].astype(BF16))
+    low_t = jnp.concatenate(low_t, axis=1)
+
+    def place(which):
         if which == 0:
-            ref[...] = dot(total, x_ref[:, :half]) * factor
+            halves[0] = dot(total, x_ref[:, :half]) * factor
         else:
-            ref[:, :start] = dot(total, x_ref[:, half:]) * factor
+            halves[1, :, :start] = dot(total, x_ref[:, half:]) * factor
+            halves[1, :, start:] = dot_nt(low_t, part_ref[...]) * factor
 
     for mine in range(2):
 
         @pl.when(core == mine)
         def _():
-            place(send_ref, 1 - mine)
-            place(keep_ref, mine)
-
-    low_t = [low_ref[...]]
-    for c in range(1, part_ref.shape[1] // rows):
-        low_t.append(received_ref[jnp.maximum(candidate_slot(slots, own, c), 0)].astype(BF16))
-    up = dot_nt(jnp.concatenate(low_t, axis=1), part_ref[...]) * factor
-
-    @pl.when(core == 0)
-    def _():
-        send_ref[:, start:] = up
-
-    @pl.when(core == 1)
-    def _():
-        keep_ref[:, start:] = up
+            place(1 - mine)
+            (sent,) = copies_of([(halves.at[1 - mine], send_hbm)], sems, 1)
+            place(mine)
+            (kept,) = copies_of([(halves.at[mine], keep_hbm)], sems, 2)
+            sent.wait()
+            kept.wait()
 
 
 def gradients(slots, received, x, parts, low, factor):
@@ -384,15 +389,58 @@
     rank = received.shape[1]
     half = (width + inner) // 2
     vm = pl.BlockSpec(memory_space=pltpu.VMEM)
+    anywhere = pl.BlockSpec(memory_space=pltpu.HBM)
     return pl.pallas_call(
         functools.partial(gradient_kernel, slots, factor),
         name="gradients",
         out_shape=(jax.ShapeDtypeStruct((rank, half), F32),) * 2,
-        in_specs=[vm] * 4,
-        out_specs=(vm, vm),
+        in_specs=[anywhere] + [vm] * 3,
+        out_specs=(anywhere, anywhere),
+        scratch_shapes=[
+            pltpu.VMEM(received.shape, F32),
+            pltpu.VMEM((2, rank, half), F32),
+            pltpu.SemaphoreType.DMA((3,)),
+        ],
         compiler_params=pltpu.CompilerParams(vmem_limit_bytes=SMALL_LIMIT),
         cost_estimate=pl.CostEstimate(flops=80_000_000, bytes_accessed=4_000_000, transcendentals=0),
     )(received, x, parts, low)
+
+
+def finish_kernel(half_ref, other_ref, down_hbm, up_hbm, whole, sems):
+    core = lax.axis_index("rep")
+    half = half_ref.shape[1]
+    width = down_hbm.shape[1]
+
+    @pl.when(core == 0)
+    def _():
+        whole[:, :half] = half_ref[...].astype(F32)
+        whole[:, half:] = other_ref[...].astype(F32)
+
+    @pl.when(core == 1)
+    def _():
+        whole[:, :half] = other_ref[...].astype(F32)
+        whole[:, half:] = half_ref[...].astype(F32)
+
+    for copy in copies_of([(whole.at[:, :width], down_hbm), (whole.at[:, width:], up_hbm)], sems):
+        copy.wait()
+
+
+def finish(half, other, width):
+    rank, columns = half.shape
+    vm = pl.BlockSpec(memory_space=pltpu.VMEM)
+    anywhere = pl.BlockSpec(memory_space=pltpu.HBM)
+    return pl.pallas_call(
+        finish_kernel,
+        name="finish",
+        out_shape=(
+            jax.ShapeDtypeStruct((rank, width), F32),
+            jax.ShapeDtypeStruct((rank, 2 * columns - width), F32),
+        ),
+        in_specs=[vm, vm],
+        out_specs=(anywhere, anywhere),
+        scratch_shapes=[pltpu.VMEM((rank, 2 * columns), F32), pltpu.SemaphoreType.DMA((2,))],
+        compiler_params=pltpu.CompilerParams(vmem_limit_bytes=SMALL_LIMIT),
+    )(half, other)
 
 
 def gather_keys(slots, block):
@@ -403,7 +451,7 @@
         columns[d] = lax.ppermute(block, "node", [(i, i + 2 * d) for i in range(slots - 2 * d)])
     blocks = []
     for d in range(slots // 2):
-        swap = [(i, i ^ 1) for i in range(2 * d, slots) if d or i % 2 == 0]
+        swap = [(i, i ^ 1) for i in range(slots)]
         blocks += [columns[d], lax.ppermute(columns[d], "node", swap)]
     return blocks
 
@@ -428,8 +476,7 @@
     return even, odd
 
 
-def sum_over_all(slots, keep, send):
-    core = lax.axis_index("rep")
+def sum_over_all(slots, keep, send, width):
     own = lax.axis_index("node")
     swap_core = [(0, 1), (1, 0)]
 
@@ -451,9 +498,7 @@
     other = swap(mine, 1)
     half = jnp.concatenate([jnp.where(odd, other, mine), jnp.where(odd, mine, other)], axis=1)
     other = lax.ppermute(half, "rep", swap_core)
-    second = core == 1
-    whole = jnp.concatenate([jnp.where(second, other, half), jnp.where(second, half, other)], axis=1)
-    return whole.astype(F32)
+    return finish(half, other, width)
 
 
 def on_device(
@@ -486,12 +531,12 @@
     received = lax.all_to_all(projected, "node", 0, 0)
     factor = (slots * lax.axis_size("rep") * rows) ** (-0.5)
     keep, send = gradients(slots, received, x, parts, low, factor)
-    whole = sum_over_all(slots, keep, send)
+    down_grad, up_grad = sum_over_all(slots, keep, send, width)
     carried = ()
     for group in range(KEY_HEADS):
         carried = attend(slots, group, carried, parents, lengths, key_blocks, value_pair, qt, gt, lse)
     attended, query_grad = carried
-    return (attended[None], query_grad[None], whole[:, :width].T, whole[:, width:])
+    return (attended[None], query_grad[None], down_grad.T, up_grad)
 
 
 def solution(mesh):

time: 113 us -> 111 us (0.982)
  blocking collectives: 19.1 us -> 13.5 us
  waiting for transfers between devices: 34.8 us -> 39.1 us
  Pallas kernels: 28.9 us -> 30.3 us
    all_to_all x1, blocking collectives: 19.1 us -> 13.5 us  [on_device(): received = lax.all_to_all(projected, 'node', 0, 0)]
    ppermute x4, waiting for transfers between devices: 0.01 us -> 3.03 us  [gather_keys(): blocks += [columns[d], lax.ppermute(columns[d], 'node', swap)]]
    ppermute x3, waiting for transfers between devices: 0.09 us -> 1.3 us  [gather_keys(): lax.ppermute(block, 'node', [(i, i + 2 * d) for i in range(slots - 2 * d)])]
  transfers between devices with their start and end apart: 15 -> 15, of which waited for: 7 -> 10; matrix products, arithmetic and copies ran while one was open for 0% -> 0% of each run, Pallas kernels for 16% -> 16%
where the time goes in v2:
time: 111 us; the launch traced here: 110 us
  waiting for transfers between devices  39.1 us (35%)
  Pallas kernels  30.3 us (27%)
  starting transfers between devices  24.1 us (22%)
  blocking collectives  13.5 us (12%)
  local copies, waits for them, and re-layouts  1.96 us (2%)
  between operations  1.19 us (1%)
    ppermute x4, waiting for transfers between devices, swap(): return lax.ppermute(x, 'node', [(i, i ^ bit) for i in range(slots)])  23.8 us
    pallas_call x4, Pallas kernels, attend(): pl.pallas_call(functools.partial(attend_kernel, slots, group, LOG2E * inv...  13.9 us
    all_to_all x1, blocking collectives, on_device(): received = lax.all_to_all(projected, 'node', 0, 0)  13.5 us
    ppermute x3, starting transfers between devices, gather_keys(): lax.ppermute(block, 'node', [(i, i + 2 * d) for i in range(slots - 2 * d)])  10.8 us
    pallas_call x1, Pallas kernels, stats(): pl.pallas_call(functools.partial(stats_kernel, slots, scale), name='stats...  10.4 us
    ppermute x1, waiting for transfers between devices, gather_values(): odd = lax.ppermute(even, 'node', [(i, i ^ 1) for i in range(slots)])  9.25 us
    ppermute x4, starting transfers between devices, gather_keys(): blocks += [columns[d], lax.ppermute(columns[d], 'node', swap)]  5.13 us
    pallas_call x1, Pallas kernels, prepare(): pl.pallas_call(prepare_kernel, name='prepare', out_shape=(jax.ShapeDtypeS...  3.84 us
  transfers between devices with their start and end apart: 15, of which 10 were waited for; matrix products, arithmetic and copies ran while one was open for 0% of the time, Pallas kernels for 16%

profile of v2, /device:TPU:0, one launch (start us, length us, event | category | flops | bytes accessed | tf_op | source)
XLA Modules:
  0.0 110.2 jit_solution(930442051072303149)
XLA Ops:
  0.6 7.0 %collective-permute-start.5 = (bf16[128,512]{1,0:T(8,128)(2,1)}, bf16[128,512]{1,0:T(8,128)(2,1)S(1)}, u32[]{:S(2)}, u32[]{:S(2)}) collective-permute-start(bf16[128,512]{1,0:T(8,128)(2,1)} %bitcast.11), channel_id=1, source_target_pairs={{0,12},{2,14},{1,13},{3,15},{16,28},{18,30},{17,29},{19,31}} | collective-permute-start | bytes 393224 | tf_op jit(solution)/shard_map/ppermute | solution.py:451
  7.6 1.3 %collective-permute-start.3 = (bf16[128,512]{1,0:T(8,128)(2,1)}, bf16[128,512]{1,0:T(8,128)(2,1)S(1)}, u32[]{:S(2)}, u32[]{:S(2)}) collective-permute-start(bf16[128,512]{1,0:T(8,128)(2,1)} %bitcast.12), channel_id=1, source_target_pairs={{0,8},{2,10},{4,12},{6,14},{1,9},{3,11},{5,13},{7,15},{16,24},{18,... | collective-permute-start | bytes 393224 | tf_op jit(solution)/shard_map/ppermute | solution.py:451
  8.9 2.5 %collective-permute-start.1 = (bf16[128,512]{1,0:T(8,128)(2,1)}, bf16[128,512]{1,0:T(8,128)(2,1)S(1)}, u32[]{:S(2)}, u32[]{:S(2)}) collective-permute-start(bf16[128,512]{1,0:T(8,128)(2,1)} %bitcast.13), channel_id=1, source_target_pairs={{0,4},{2,6},{4,8},{6,10},{8,12},{10,14},{1,5},{3,7},{5,9},{7,11},{... | collective-permute-start | bytes 393224 | tf_op jit(solution)/shard_map/ppermute | solution.py:451
  11.4 1.6 %collective-permute-start = (bf16[128,512]{1,0:T(8,128)(2,1)}, bf16[128,512]{1,0:T(8,128)(2,1)S(1)}, u32[]{:S(2)}, u32[]{:S(2)}) collective-permute-start(bf16[128,512]{1,0:T(8,128)(2,1)} %bitcast.14), channel_id=1, source_target_pairs={{0,2},{2,0},{4,6},{6,4},{8,10},{10,8},{12,14},{14,12},{1,3},{3,1},... | collective-permute-start | bytes 393224 | tf_op jit(solution)/shard_map/ppermute | solution.py:455
  13.0 0.5 collective-permute-start.6
  13.5 1.1 %collective-permute-done.3.refs_6_ = bf16[128,512]{1,0:T(8,128)(2,1)S(1)} collective-permute-done((bf16[128,512]{1,0:T(8,128)(2,1)}, bf16[128,512]{1,0:T(8,128)(2,1)S(1)}, u32[]{:S(2)}, u32[]{:S(2)}) %collective-permute-start.3) | collective-permute-done | bytes 131104 | tf_op jit(solution)/shard_map/ppermute | solution.py:451
  14.7 1.5 %collective-permute-start.4 = (bf16[128,512]{1,0:T(8,128)(2,1)S(1)}, bf16[128,512]{1,0:T(8,128)(2,1)S(1)}, u32[]{:S(2)}, u32[]{:S(2)}) collective-permute-start(bf16[128,512]{1,0:T(8,128)(2,1)S(1)} %collective-permute-done.3.refs_6_), channel_id=1, source_target_pairs={{0,2},{2,0},{4,6},{6,4},{8,10},{10,8},{12,14},{14,12},{1,3},{3,1},... | collective-permute-start | bytes 393224 | tf_op jit(solution)/shard_map/ppermute | solution.py:455
  16.3 1.5 %collective-permute-start.2 = (bf16[128,512]{1,0:T(8,128)(2,1)S(1)}, bf16[128,512]{1,0:T(8,128)(2,1)S(1)}, u32[]{:S(2)}, u32[]{:S(2)}) collective-permute-start(bf16[128,512]{1,0:T(8,128)(2,1)S(1)} %collective-permute-done.1.refs_4_), channel_id=1, source_target_pairs={{0,2},{2,0},{4,6},{6,4},{8,10},{10,8},{12,14},{14,12},{1,3},{3,1},... | collective-permute-start | bytes 393224 | tf_op jit(solution)/shard_map/ppermute | solution.py:455
  17.9 3.8 %prepare.1 = (bf16[4,128,512]{2,1,0:T(8,128)(2,1)}, bf16[32,128]{1,0:T(8,128)(2,1)}, bf16[128,2560]{1,0:T(8,128)(2,1)}, bf16[128,2560]{1,0:T(8,128)(2,1)}) custom-call(s32[1,8]{1,0:T(1,128)} %refs_1_.9, bf16[128,5120]{1,0:T(8,128)(2,1)} %bitcast.9, bf16[32,5120]{1,0:T(8,128)(2,1)} %bitcast.24, bf16[32,512]{1,0:T(8,128)(2,1)} %refs_12_.1, ...), custom_call_target="tpu_custom_call" | custom-call | flops 100000000 | bytes 6000000 | tf_op jit(solution)/shard_map/prepare/pallas_call | solution.py:117
  21.8 1.6 %collective-permute-done.4.refs_7_ = bf16[128,512]{1,0:T(8,128)(2,1)S(1)} collective-permute-done((bf16[128,512]{1,0:T(8,128)(2,1)S(1)}, bf16[128,512]{1,0:T(8,128)(2,1)S(1)}, u32[]{:S(2)}, u32[]{:S(2)}) %collective-permute-start.4) | collective-permute-done | bytes 131104 | tf_op jit(solution)/shard_map/ppermute | solution.py:455
  23.4 1.4 %collective-permute-done.2.refs_5_ = bf16[128,512]{1,0:T(8,128)(2,1)S(1)} collective-permute-done((bf16[128,512]{1,0:T(8,128)(2,1)S(1)}, bf16[128,512]{1,0:T(8,128)(2,1)S(1)}, u32[]{:S(2)}, u32[]{:S(2)}) %collective-permute-start.2) | collective-permute-done | bytes 131104 | tf_op jit(solution)/shard_map/ppermute | solution.py:455
  24.8 0.6 copy-done.16
  25.4 10.4 %stats.1 = (f32[8,32,128]{2,1,0:T(8,128)}, bf16[512,1024]{1,0:T(8,128)(2,1)}, f32[1,2560]{1,0:T(1,128)}) custom-call(s32[1,8]{1,0:T(1,128)} %refs_0_.9, s32[1,8]{1,0:T(1,128)} %refs_1_.9, bf16[128,512]{1,0:T(8,128)(2,1)} %bitcast.15, bf16[128,512]{1,0:T(8,128)(2,1)} %copy-done.10, bf16[128,512]{1,0:T(8,128)(2,1)} %copy-done.8, bf16[128,512]{1,0:T(8,128)(2,1)} %copy-done.16, ...), custom_call_target="tpu_custom_call" | custom-call | flops 2000000000 | bytes 5000000 | tf_op jit(solution)/shard_map/stats/pallas_call | solution.py:231
  35.9 13.5 %all_to_all.10.received_hbm = f32[8,32,128]{2,1,0:T(8,128)S(1)} all-to-all(f32[8,32,128]{2,1,0:T(8,128)} %get-tuple-element.36), channel_id=1, replica_groups=mesh['groups'=2,'node'=8,'rep'=2] {'node'}, dimensions={0} | all-to-all | bytes 262144 | tf_op jit(solution)/shard_map/all_to_all | solution.py:531
  49.3 1.2 %copy-done.18 = bf16[512,1024]{1,0:T(8,128)(2,1)S(1)} copy-done((bf16[512,1024]{1,0:T(8,128)(2,1)S(1)}, bf16[512,1024]{1,0:T(8,128)(2,1)}, u32[]{:S(2)}) %copy-start.18) | copy-done | bytes 1048600
  50.6 1.2 %gradients.1 = (f32[32,2816]{1,0:T(8,128)S(1)}, f32[32,2816]{1,0:T(8,128)S(1)}) custom-call(f32[8,32,128]{2,1,0:T(8,128)S(1)} %all_to_all.10.received_hbm, bf16[128,5120]{1,0:T(8,128)(2,1)S(1)} %bitcast.10, bf16[512,1024]{1,0:T(8,128)(2,1)S(1)} %copy-done.18, bf16[32,128]{1,0:T(8,128)(2,1)S(1)} %copy-done.21), custom_call_target="tpu_custom_call" | custom-call | flops 80000000 | bytes 4000000 | tf_op jit(solution)/shard_map/gradients/pallas_call | solution.py:393
  51.9 1.6 %collective-permute-done.8 = f32[32,2816]{1,0:T(8,128)S(1)} collective-permute-done((f32[32,2816]{1,0:T(8,128)S(1)}, f32[32,2816]{1,0:T(8,128)S(1)}, u32[]{:S(2)}, u32[]{:S(2)}) %collective-permute-start.8) | collective-permute-done | bytes 360480 | tf_op jit(solution)/shard_map/ppermute | solution.py:486
  53.8 0.3 collective-permute-start.9
  54.1 4.4 %collective-permute-done.9 = bf16[32,1408]{1,0:T(8,128)(2,1)S(1)} collective-permute-done((bf16[32,1408]{1,0:T(8,128)(2,1)S(1)}, bf16[32,1408]{1,0:T(8,128)(2,1)S(1)}, u32[]{:S(2)}, u32[]{:S(2)}) %collective-permute-start.9) | collective-permute-done | bytes 90144 | tf_op jit(solution)/shard_map/ppermute | solution.py:484
  58.6 3.7 %all-to-all-start = ((bf16[4,128,512]{2,1,0:T(8,128)(2,1)}), bf16[4,128,512]{2,1,0:T(8,128)(2,1)S(1)}, u32[]{:S(2)}, u32[]{:S(2)}) async-start(bf16[4,128,512]{2,1,0:T(8,128)(2,1)} %get-tuple-element.23), calls=%async_computation | async-start | bytes 1048576 | tf_op jit(solution)/shard_map/all_to_all | solution.py:472
  62.3 0.8 collective-permute-done.10
  63.2 1.9 %collective-permute-start.11 = (bf16[32,1408]{1,0:T(8,128)(2,1)S(1)}, bf16[32,1408]{1,0:T(8,128)(2,1)S(1)}, u32[]{:S(2)}, u32[]{:S(2)}) collective-permute-start(bf16[32,1408]{1,0:T(8,128)(2,1)S(1)} %add_convert_fusion.1), channel_id=1, source_target_pairs={{0,8},{2,10},{4,12},{6,14},{8,0},{10,2},{12,4},{14,6},{1,9},{3,11}... | collective-permute-start | bytes 270344 | tf_op jit(solution)/shard_map/ppermute | solution.py:484
  65.1 15.1 %collective-permute-done.11 = bf16[32,1408]{1,0:T(8,128)(2,1)S(1)} collective-permute-done((bf16[32,1408]{1,0:T(8,128)(2,1)S(1)}, bf16[32,1408]{1,0:T(8,128)(2,1)S(1)}, u32[]{:S(2)}, u32[]{:S(2)}) %collective-permute-start.11) | collective-permute-done | bytes 90144 | tf_op jit(solution)/shard_map/ppermute | solution.py:484
  80.2 1.1 collective-permute-start.12
  81.2 1.0 collective-permute-start.7
  82.3 3.5 %collective-permute-done.12 = bf16[32,1408]{1,0:T(8,128)(2,1)S(1)} collective-permute-done((bf16[32,1408]{1,0:T(8,128)(2,1)S(1)}, bf16[32,1408]{1,0:T(8,128)(2,1)S(1)}, u32[]{:S(2)}, u32[]{:S(2)}) %collective-permute-start.12) | collective-permute-done | bytes 90144 | tf_op jit(solution)/shard_map/ppermute | solution.py:484
  85.9 9.3 %collective-permute-done.7.refs_11_ = bf16[4,128,512]{2,1,0:T(8,128)(2,1)S(1)} collective-permute-done((bf16[4,128,512]{2,1,0:T(8,128)(2,1)S(1)}, bf16[4,128,512]{2,1,0:T(8,128)(2,1)S(1)}, u32[]{:S(2)}, u32[]{:S(2)}) %collective-permute-start.7) | collective-permute-done | bytes 524320 | tf_op jit(solution)/shard_map/ppermute | solution.py:475
  95.2 3.5 %attend.4 = (bf16[128,2560]{1,0:T(8,128)(2,1)}, bf16[128,2560]{1,0:T(8,128)(2,1)}) custom-call(s32[1,8]{1,0:T(1,128)S(1)} %copy-done.22, s32[1,8]{1,0:T(1,128)S(1)} %copy-done.20, bf16[128,512]{1,0:T(8,128)(2,1)S(1)} %bitcast.16, bf16[128,512]{1,0:T(8,128)(2,1)S(1)} %copy-done.11, bf16[128,512]{1,0:T(8,128)(2,1)S(1)} %copy-done.9, ...), custom_call_target="tpu_custom_call" | custom-call | flops 800000000 | bytes 1500000 | tf_op jit(solution)/shard_map/attend/pallas_call | solution.py:325
  98.7 3.5 %attend.5 = (bf16[128,2560]{1,0:T(8,128)(2,1)}, bf16[128,2560]{1,0:T(8,128)(2,1)}) custom-call(s32[1,8]{1,0:T(1,128)S(1)} %copy-done.22, s32[1,8]{1,0:T(1,128)S(1)} %copy-done.20, bf16[128,512]{1,0:T(8,128)(2,1)S(1)} %bitcast.17, bf16[128,512]{1,0:T(8,128)(2,1)S(1)} %copy-done.11, ...), custom_call_target="tpu_custom_call", output_to_operand_aliasing={{0}: (15, {}), {1}: (16, {})} | custom-call | flops 800000000 | bytes 1500000 | tf_op jit(solution)/shard_map/attend/pallas_call | solution.py:325
  102.2 3.5 %attend.6 = (bf16[128,2560]{1,0:T(8,128)(2,1)}, bf16[128,2560]{1,0:T(8,128)(2,1)}) custom-call(s32[1,8]{1,0:T(1,128)S(1)} %copy-done.22, s32[1,8]{1,0:T(1,128)S(1)} %copy-done.20, bf16[128,512]{1,0:T(8,128)(2,1)S(1)} %bitcast.18, bf16[128,512]{1,0:T(8,128)(2,1)S(1)} %copy-done.11, ...), custom_call_target="tpu_custom_call", output_to_operand_aliasing={{0}: (15, {}), {1}: (16, {})} | custom-call | flops 800000000 | bytes 1500000 | tf_op jit(solution)/shard_map/attend/pallas_call | solution.py:325
  105.7 3.5 %attend.7 = (bf16[128,2560]{1,0:T(8,128)(2,1)}, bf16[128,2560]{1,0:T(8,128)(2,1)}) custom-call(s32[1,8]{1,0:T(1,128)S(1)} %copy-done.22, s32[1,8]{1,0:T(1,128)S(1)} %copy-done.20, bf16[128,512]{1,0:T(8,128)(2,1)S(1)} %bitcast.19, bf16[128,512]{1,0:T(8,128)(2,1)S(1)} %copy-done.11, ...), custom_call_target="tpu_custom_call", output_to_operand_aliasing={{0}: (15, {}), {1}: (16, {})} | custom-call | flops 800000000 | bytes 1500000 | tf_op jit(solution)/shard_map/attend/pallas_call | solution.py:325
  109.1 0.9 finish.1
  (60 shorter events, 0.7 us)
Async XLA Ops:
  0.6 12.4 %collective-permute-start.5 = (bf16[128,512]{1,0:T(8,128)(2,1)}, bf16[128,512]{1,0:T(8,128)(2,1)S(1)}, u32[]{:S(2)}, u32[]{:S(2)}) collective-permute-start(bf16[128,512]{1,0:T(8,128)(2,1)} %bitcast.11), channel_id=1, source_target_pairs={{0,12},{2,14},{1,13},{3,15},{16,28},{18,30},{17,29},{19,31}} | collective-permute-start | bytes 393224 | tf_op jit(solution)/shard_map/ppermute | solution.py:451
  7.6 7.0 %collective-permute-start.3 = (bf16[128,512]{1,0:T(8,128)(2,1)}, bf16[128,512]{1,0:T(8,128)(2,1)S(1)}, u32[]{:S(2)}, u32[]{:S(2)}) collective-permute-start(bf16[128,512]{1,0:T(8,128)(2,1)} %bitcast.12), channel_id=1, source_target_pairs={{0,8},{2,10},{4,12},{6,14},{1,9},{3,11},{5,13},{7,15},{16,24},{18,... | collective-permute-start | bytes 393224 | tf_op jit(solution)/shard_map/ppermute | solution.py:451
  8.9 7.4 %collective-permute-start.1 = (bf16[128,512]{1,0:T(8,128)(2,1)}, bf16[128,512]{1,0:T(8,128)(2,1)S(1)}, u32[]{:S(2)}, u32[]{:S(2)}) collective-permute-start(bf16[128,512]{1,0:T(8,128)(2,1)} %bitcast.13), channel_id=1, source_target_pairs={{0,4},{2,6},{4,8},{6,10},{8,12},{10,14},{1,5},{3,7},{5,9},{7,11},{... | collective-permute-start | bytes 393224 | tf_op jit(solution)/shard_map/ppermute | solution.py:451
  11.4 10.3 %collective-permute-start = (bf16[128,512]{1,0:T(8,128)(2,1)}, bf16[128,512]{1,0:T(8,128)(2,1)S(1)}, u32[]{:S(2)}, u32[]{:S(2)}) collective-permute-start(bf16[128,512]{1,0:T(8,128)(2,1)} %bitcast.14), channel_id=1, source_target_pairs={{0,2},{2,0},{4,6},{6,4},{8,10},{10,8},{12,14},{14,12},{1,3},{3,1},... | collective-permute-start | bytes 393224 | tf_op jit(solution)/shard_map/ppermute | solution.py:455
  13.0 8.7 %copy-start.4 = (bf16[128,512]{1,0:T(8,128)(2,1)}, bf16[128,512]{1,0:T(8,128)(2,1)S(1)}, u32[]{:S(2)}) copy-start(bf16[128,512]{1,0:T(8,128)(2,1)S(1)} %collective-permute-done.5.refs_8_) | copy-start | bytes 393220
  13.0 8.7 %collective-permute-start.6 = (bf16[128,512]{1,0:T(8,128)(2,1)S(1)}, bf16[128,512]{1,0:T(8,128)(2,1)S(1)}, u32[]{:S(2)}, u32[]{:S(2)}) collective-permute-start(bf16[128,512]{1,0:T(8,128)(2,1)S(1)} %collective-permute-done.5.refs_8_), channel_id=1, source_target_pairs={{0,2},{2,0},{4,6},{6,4},{8,10},{10,8},{12,14},{14,12},{1,3},{3,1},... | collective-permute-start | bytes 393224 | tf_op jit(solution)/shard_map/ppermute | solution.py:455
  14.7 7.1 %copy-start.6 = (bf16[128,512]{1,0:T(8,128)(2,1)}, bf16[128,512]{1,0:T(8,128)(2,1)S(1)}, u32[]{:S(2)}) copy-start(bf16[128,512]{1,0:T(8,128)(2,1)S(1)} %collective-permute-done.3.refs_6_) | copy-start | bytes 393220
  14.7 8.7 %collective-permute-start.4 = (bf16[128,512]{1,0:T(8,128)(2,1)S(1)}, bf16[128,512]{1,0:T(8,128)(2,1)S(1)}, u32[]{:S(2)}, u32[]{:S(2)}) collective-permute-start(bf16[128,512]{1,0:T(8,128)(2,1)S(1)} %collective-permute-done.3.refs_6_), channel_id=1, source_target_pairs={{0,2},{2,0},{4,6},{6,4},{8,10},{10,8},{12,14},{14,12},{1,3},{3,1},... | collective-permute-start | bytes 393224 | tf_op jit(solution)/shard_map/ppermute | solution.py:455
  16.3 8.5 %collective-permute-start.2 = (bf16[128,512]{1,0:T(8,128)(2,1)S(1)}, bf16[128,512]{1,0:T(8,128)(2,1)S(1)}, u32[]{:S(2)}, u32[]{:S(2)}) collective-permute-start(bf16[128,512]{1,0:T(8,128)(2,1)S(1)} %collective-permute-done.1.refs_4_), channel_id=1, source_target_pairs={{0,2},{2,0},{4,6},{6,4},{8,10},{10,8},{12,14},{14,12},{1,3},{3,1},... | collective-permute-start | bytes 393224 | tf_op jit(solution)/shard_map/ppermute | solution.py:455
  25.4 23.9 %copy-start.2 = (bf16[1,128,5120]{2,1,0:T(8,128)(2,1)S(1)}, bf16[1,128,5120]{2,1,0:T(8,128)(2,1)}, u32[]{:S(2)}) copy-start(bf16[1,128,5120]{2,1,0:T(8,128)(2,1)} %param.9) | copy-start | bytes 3932164
  25.4 23.9 %copy-start.21 = (bf16[32,128]{1,0:T(8,128)(2,1)S(1)}, bf16[32,128]{1,0:T(8,128)(2,1)}, u32[]{:S(2)}) copy-start(bf16[32,128]{1,0:T(8,128)(2,1)} %get-tuple-element.26.refs_13_.low_ref) | copy-start | bytes 24580
  51.8 1.7 %collective-permute-start.8 = (f32[32,2816]{1,0:T(8,128)S(1)}, f32[32,2816]{1,0:T(8,128)S(1)}, u32[]{:S(2)}, u32[]{:S(2)}) collective-permute-start(f32[32,2816]{1,0:T(8,128)S(1)} %get-tuple-element.39), channel_id=1, source_target_pairs={{0,1},{1,0},{2,3},{3,2},{4,5},{5,4},{6,7},{7,6},{8,9},{9,8},{10,11... | collective-permute-start | bytes 1081352 | tf_op jit(solution)/shard_map/ppermute | solution.py:486
  53.6 41.5 %copy-start = (bf16[128,2560]{1,0:T(8,128)(2,1)S(1)}, bf16[128,2560]{1,0:T(8,128)(2,1)}, u32[]{:S(2)}) copy-start(bf16[128,2560]{1,0:T(8,128)(2,1)} %get-tuple-element.24.refs_10_.refs_12_) | copy-start | bytes 1966084
  53.6 41.5 %copy-start.1 = (bf16[128,2560]{1,0:T(8,128)(2,1)S(1)}, bf16[128,2560]{1,0:T(8,128)(2,1)}, u32[]{:S(2)}) copy-start(bf16[128,2560]{1,0:T(8,128)(2,1)} %get-tuple-element.25.refs_11_.refs_13_) | copy-start | bytes 1966084
  53.7 41.5 %copy-start.3 = (bf16[1,128,512]{2,1,0:T(8,128)(2,1)S(1)}, bf16[1,128,512]{2,1,0:T(8,128)(2,1)}, u32[]{:S(2)}) copy-start(bf16[1,128,512]{2,1,0:T(8,128)(2,1)} %param.11) | copy-start | bytes 393220
  53.7 41.5 %copy-start.5 = (bf16[128,512]{1,0:T(8,128)(2,1)S(1)}, bf16[128,512]{1,0:T(8,128)(2,1)}, u32[]{:S(2)}) copy-start(bf16[128,512]{1,0:T(8,128)(2,1)} %copy-done.4) | copy-start | bytes 393220
  53.7 41.5 %copy-start.7 = (bf16[128,512]{1,0:T(8,128)(2,1)S(1)}, bf16[128,512]{1,0:T(8,128)(2,1)}, u32[]{:S(2)}) copy-start(bf16[128,512]{1,0:T(8,128)(2,1)} %copy-done.6) | copy-start | bytes 393220
  53.7 41.5 %copy-start.9 = (bf16[128,512]{1,0:T(8,128)(2,1)S(1)}, bf16[128,512]{1,0:T(8,128)(2,1)}, u32[]{:S(2)}) copy-start(bf16[128,512]{1,0:T(8,128)(2,1)} %copy-done.8) | copy-start | bytes 393220
  53.7 41.5 %copy-start.11 = (bf16[128,512]{1,0:T(8,128)(2,1)S(1)}, bf16[128,512]{1,0:T(8,128)(2,1)}, u32[]{:S(2)}) copy-start(bf16[128,512]{1,0:T(8,128)(2,1)} %copy-done.10) | copy-start | bytes 393220
  53.7 41.5 %copy-start.13 = (bf16[128,512]{1,0:T(8,128)(2,1)S(1)}, bf16[128,512]{1,0:T(8,128)(2,1)}, u32[]{:S(2)}) copy-start(bf16[128,512]{1,0:T(8,128)(2,1)} %copy-done.12) | copy-start | bytes 393220
  53.7 41.5 %copy-start.15 = (bf16[128,512]{1,0:T(8,128)(2,1)S(1)}, bf16[128,512]{1,0:T(8,128)(2,1)}, u32[]{:S(2)}) copy-start(bf16[128,512]{1,0:T(8,128)(2,1)} %copy-done.14) | copy-start | bytes 393220
  53.7 41.5 %copy-start.17 = (bf16[128,512]{1,0:T(8,128)(2,1)S(1)}, bf16[128,512]{1,0:T(8,128)(2,1)}, u32[]{:S(2)}) copy-start(bf16[128,512]{1,0:T(8,128)(2,1)} %copy-done.16) | copy-start | bytes 393220
  53.7 41.5 %copy-start.19 = (f32[1,2560]{1,0:T(1,128)S(1)}, f32[1,2560]{1,0:T(1,128)}, u32[]{:S(2)}) copy-start(f32[1,2560]{1,0:T(1,128)} %get-tuple-element.27.refs_14_) | copy-start | bytes 30724
  53.7 41.5 %copy-start.20 = (s32[1,8]{1,0:T(1,128)S(1)}, s32[1,8]{1,0:T(1,128)}, u32[]{:S(2)}) copy-start(s32[1,8]{1,0:T(1,128)} %refs_1_.9) | copy-start | bytes 100
  53.8 41.4 %copy-start.22 = (s32[1,8]{1,0:T(1,128)S(1)}, s32[1,8]{1,0:T(1,128)}, u32[]{:S(2)}) copy-start(s32[1,8]{1,0:T(1,128)} %refs_0_.9) | copy-start | bytes 100
  53.8 4.7 %collective-permute-start.9 = (bf16[32,1408]{1,0:T(8,128)(2,1)S(1)}, bf16[32,1408]{1,0:T(8,128)(2,1)S(1)}, u32[]{:S(2)}, u32[]{:S(2)}) collective-permute-start(bf16[32,1408]{1,0:T(8,128)(2,1)S(1)} %select_convert_fusion), channel_id=1, source_target_pairs={{0,2},{2,0},{4,6},{6,4},{8,10},{10,8},{12,14},{14,12},{1,3},{3,1},... | collective-permute-start | bytes 270344 | tf_op jit(solution)/shard_map/ppermute | solution.py:484
  58.5 4.6 %collective-permute-start.10 = (bf16[32,1408]{1,0:T(8,128)(2,1)S(1)}, bf16[32,1408]{1,0:T(8,128)(2,1)S(1)}, u32[]{:S(2)}, u32[]{:S(2)}) collective-permute-start(bf16[32,1408]{1,0:T(8,128)(2,1)S(1)} %add_convert_fusion.2), channel_id=1, source_target_pairs={{0,4},{2,6},{4,0},{6,2},{8,12},{10,14},{12,8},{14,10},{1,5},{3,7},... | collective-permute-start | bytes 270344 | tf_op jit(solution)/shard_map/ppermute | solution.py:484
  58.6 22.6 %all-to-all-start = ((bf16[4,128,512]{2,1,0:T(8,128)(2,1)}), bf16[4,128,512]{2,1,0:T(8,128)(2,1)S(1)}, u32[]{:S(2)}, u32[]{:S(2)}) async-start(bf16[4,128,512]{2,1,0:T(8,128)(2,1)} %get-tuple-element.23), calls=%async_computation | async-start | bytes 1048576 | tf_op jit(solution)/shard_map/all_to_all | solution.py:472
  63.2 17.0 %collective-permute-start.11 = (bf16[32,1408]{1,0:T(8,128)(2,1)S(1)}, bf16[32,1408]{1,0:T(8,128)(2,1)S(1)}, u32[]{:S(2)}, u32[]{:S(2)}) collective-permute-start(bf16[32,1408]{1,0:T(8,128)(2,1)S(1)} %add_convert_fusion.1), channel_id=1, source_target_pairs={{0,8},{2,10},{4,12},{6,14},{8,0},{10,2},{12,4},{14,6},{1,9},{3,11}... | collective-permute-start | bytes 270344 | tf_op jit(solution)/shard_map/ppermute | solution.py:484
  80.2 5.6 %collective-permute-start.12 = (bf16[32,1408]{1,0:T(8,128)(2,1)S(1)}, bf16[32,1408]{1,0:T(8,128)(2,1)S(1)}, u32[]{:S(2)}, u32[]{:S(2)}) collective-permute-start(bf16[32,1408]{1,0:T(8,128)(2,1)S(1)} %add_convert_fusion), channel_id=1, source_target_pairs={{0,2},{2,0},{4,6},{6,4},{8,10},{10,8},{12,14},{14,12},{1,3},{3,1},... | collective-permute-start | bytes 270344 | tf_op jit(solution)/shard_map/ppermute | solution.py:484
  81.2 13.9 %collective-permute-start.7 = (bf16[4,128,512]{2,1,0:T(8,128)(2,1)S(1)}, bf16[4,128,512]{2,1,0:T(8,128)(2,1)S(1)}, u32[]{:S(2)}, u32[]{:S(2)}) collective-permute-start(bf16[4,128,512]{2,1,0:T(8,128)(2,1)S(1)} %all-to-all-done.refs_10_), channel_id=1, source_target_pairs={{0,2},{2,0},{4,6},{6,4},{8,10},{10,8},{12,14},{14,12},{1,3},{3,1},... | collective-permute-start | bytes 1572872 | tf_op jit(solution)/shard_map/ppermute | solution.py:475
  85.8 23.4 %collective-permute-start.13 = (bf16[32,2816]{1,0:T(8,128)(2,1)S(1)}, bf16[32,2816]{1,0:T(8,128)(2,1)S(1)}, u32[]{:S(2)}, u32[]{:S(2)}) collective-permute-start(bf16[32,2816]{1,0:T(8,128)(2,1)S(1)} %pad_maximum_fusion.half_ref), channel_id=1, source_target_pairs={{0,1},{1,0},{2,3},{3,2},{4,5},{5,4},{6,7},{7,6},{8,9},{9,8},{10,11... | collective-permute-start | bytes 540680 | tf_op jit(solution)/shard_map/ppermute | solution.py:500
  (6 other events, 14.8 us)

commit v3 on v2

--- a/solution.py
+++ b/solution.py
@@ -347,13 +347,15 @@
     )(parents, lengths, *key_blocks, *value_pair, qt, gt, lse, *carried)
 
 
-def gradient_kernel(slots, factor, received_hbm, x_ref, part_ref, low_ref, keep_hbm, send_hbm, received_ref, halves, sems):
+def gradient_kernel(
+    slots, factor, received_hbm, x_ref, part_hbm, low_ref, keep_ref, send_hbm, received_ref, part_ref, send_ref, sems
+):
     width = x_ref.shape[1]
     core = lax.axis_index("rep")
     own = lax.axis_index("node")
-    half = halves.shape[2]
+    half = keep_ref.shape[1]
     start = width - half
-    (arrival,) = copies_of([(received_hbm, received_ref)], sems)
+    arrival, parts = copies_of([(received_hbm, received_ref), (part_hbm, part_ref)], sems)
     arrival.wait()
     total = received_ref[own]
     for slot in range(slots):
@@ -364,23 +366,26 @@
         low_t.append(received_ref[jnp.maximum(candidate_slot(slots, own, c), 0)].astype(BF16))
     low_t = jnp.concatenate(low_t, axis=1)
 
-    def place(which):
-        if which == 0:
-            halves[0] = dot(total, x_ref[:, :half]) * factor
-        else:
-            halves[1, :, :start] = dot(total, x_ref[:, half:]) * factor
-            halves[1, :, start:] = dot_nt(low_t, part_ref[...]) * factor
-
-    for mine in range(2):
-
-        @pl.when(core == mine)
-        def _():
-            place(1 - mine)
-            (sent,) = copies_of([(halves.at[1 - mine], send_hbm)], sems, 1)
-            place(mine)
-            (kept,) = copies_of([(halves.at[mine], keep_hbm)], sems, 2)
-            sent.wait()
-            kept.wait()
+    def place(ref):
+        ref[...] = dot(total, x_ref[:, :half]) * factor
+
+    @pl.when(core == 1)
+    def _():
+        place(send_ref)
+        (sent,) = copies_of([(send_ref, send_hbm)], sems, 2)
+        parts.wait()
+        keep_ref[:, start:] = dot_nt(low_t, part_ref[...]) * factor
+        keep_ref[:, :start] = dot(total, x_ref[:, half:]) * factor
+        sent.wait()
+
+    @pl.when(core == 0)
+    def _():
+        send_ref[:, :start] = dot(total, x_ref[:, half:]) * factor
+        parts.wait()
+        send_ref[:, start:] = dot_nt(low_t, part_ref[...]) * factor
+        (sent,) = copies_of([(send_ref, send_hbm)], sems, 2)
+        place(keep_ref)
+        sent.wait()
 
 
 def gradients(slots, received, x, parts, low, factor):
@@ -394,11 +399,12 @@
         functools.partial(gradient_kernel, slots, factor),
         name="gradients",
         out_shape=(jax.ShapeDtypeStruct((rank, half), F32),) * 2,
-        in_specs=[anywhere] + [vm] * 3,
-        out_specs=(anywhere, anywhere),
+        in_specs=[anywhere, vm, anywhere, vm],
+        out_specs=(vm, anywhere),
         scratch_shapes=[
             pltpu.VMEM(received.shape, F32),
-            pltpu.VMEM((2, rank, half), F32),
+            pltpu.VMEM(parts.shape, BF16),
+            pltpu.VMEM((rank, half), F32),
             pltpu.SemaphoreType.DMA((3,)),
         ],
         compiler_params=pltpu.CompilerParams(vmem_limit_bytes=SMALL_LIMIT),

time: 111 us -> 111 us (level)
  no operation moved by 1% of the time
where the time goes in v3:
time: 111 us; the launch traced here: 110 us
  waiting for transfers between devices  39.1 us (35%)
  Pallas kernels  30.4 us (27%)
  starting transfers between devices  24.1 us (22%)
  blocking collectives  13.5 us (12%)
  local copies, waits for them, and re-layouts  1.96 us (2%)
  between operations  1.19 us (1%)
    ppermute x4, waiting for transfers between devices, swap(): return lax.ppermute(x, 'node', [(i, i ^ bit) for i in range(slots)])  23.8 us
    pallas_call x4, Pallas kernels, attend(): pl.pallas_call(functools.partial(attend_kernel, slots, group, LOG2E * inv...  13.9 us
    all_to_all x1, blocking collectives, on_device(): received = lax.all_to_all(projected, 'node', 0, 0)  13.5 us
    ppermute x3, starting transfers between devices, gather_keys(): lax.ppermute(block, 'node', [(i, i + 2 * d) for i in range(slots - 2 * d)])  10.8 us
    pallas_call x1, Pallas kernels, stats(): pl.pallas_call(functools.partial(stats_kernel, slots, scale), name='stats...  10.4 us
    ppermute x1, waiting for transfers between devices, gather_values(): odd = lax.ppermute(even, 'node', [(i, i ^ 1) for i in range(slots)])  9.25 us
    ppermute x4, starting transfers between devices, gather_keys(): blocks += [columns[d], lax.ppermute(columns[d], 'node', swap)]  5.13 us
    pallas_call x1, Pallas kernels, prepare(): pl.pallas_call(prepare_kernel, name='prepare', out_shape=(jax.ShapeDtypeS...  3.84 us
  transfers between devices with their start and end apart: 15, of which 10 were waited for; matrix products, arithmetic and copies ran while one was open for 0% of the time, Pallas kernels for 16%

profile of v3, /device:TPU:0, one launch (start us, length us, event | category | flops | bytes accessed | tf_op | source)
XLA Modules:
  0.0 110.3 jit_solution(14499763316981781702)
XLA Ops:
  0.6 7.0 %collective-permute-start.5 = (bf16[128,512]{1,0:T(8,128)(2,1)}, bf16[128,512]{1,0:T(8,128)(2,1)S(1)}, u32[]{:S(2)}, u32[]{:S(2)}) collective-permute-start(bf16[128,512]{1,0:T(8,128)(2,1)} %bitcast.11), channel_id=1, source_target_pairs={{0,12},{2,14},{1,13},{3,15},{16,28},{18,30},{17,29},{19,31}} | collective-permute-start | bytes 393224 | tf_op jit(solution)/shard_map/ppermute | solution.py:457
  7.6 1.3 %collective-permute-start.3 = (bf16[128,512]{1,0:T(8,128)(2,1)}, bf16[128,512]{1,0:T(8,128)(2,1)S(1)}, u32[]{:S(2)}, u32[]{:S(2)}) collective-permute-start(bf16[128,512]{1,0:T(8,128)(2,1)} %bitcast.12), channel_id=1, source_target_pairs={{0,8},{2,10},{4,12},{6,14},{1,9},{3,11},{5,13},{7,15},{16,24},{18,... | collective-permute-start | bytes 393224 | tf_op jit(solution)/shard_map/ppermute | solution.py:457
  8.9 2.5 %collective-permute-start.1 = (bf16[128,512]{1,0:T(8,128)(2,1)}, bf16[128,512]{1,0:T(8,128)(2,1)S(1)}, u32[]{:S(2)}, u32[]{:S(2)}) collective-permute-start(bf16[128,512]{1,0:T(8,128)(2,1)} %bitcast.13), channel_id=1, source_target_pairs={{0,4},{2,6},{4,8},{6,10},{8,12},{10,14},{1,5},{3,7},{5,9},{7,11},{... | collective-permute-start | bytes 393224 | tf_op jit(solution)/shard_map/ppermute | solution.py:457
  11.4 1.6 %collective-permute-start = (bf16[128,512]{1,0:T(8,128)(2,1)}, bf16[128,512]{1,0:T(8,128)(2,1)S(1)}, u32[]{:S(2)}, u32[]{:S(2)}) collective-permute-start(bf16[128,512]{1,0:T(8,128)(2,1)} %bitcast.14), channel_id=1, source_target_pairs={{0,2},{2,0},{4,6},{6,4},{8,10},{10,8},{12,14},{14,12},{1,3},{3,1},... | collective-permute-start | bytes 393224 | tf_op jit(solution)/shard_map/ppermute | solution.py:461
  13.0 0.5 collective-permute-start.6
  13.5 1.1 %collective-permute-done.3.refs_6_ = bf16[128,512]{1,0:T(8,128)(2,1)S(1)} collective-permute-done((bf16[128,512]{1,0:T(8,128)(2,1)}, bf16[128,512]{1,0:T(8,128)(2,1)S(1)}, u32[]{:S(2)}, u32[]{:S(2)}) %collective-permute-start.3) | collective-permute-done | bytes 131104 | tf_op jit(solution)/shard_map/ppermute | solution.py:457
  14.7 1.5 %collective-permute-start.4 = (bf16[128,512]{1,0:T(8,128)(2,1)S(1)}, bf16[128,512]{1,0:T(8,128)(2,1)S(1)}, u32[]{:S(2)}, u32[]{:S(2)}) collective-permute-start(bf16[128,512]{1,0:T(8,128)(2,1)S(1)} %collective-permute-done.3.refs_6_), channel_id=1, source_target_pairs={{0,2},{2,0},{4,6},{6,4},{8,10},{10,8},{12,14},{14,12},{1,3},{3,1},... | collective-permute-start | bytes 393224 | tf_op jit(solution)/shard_map/ppermute | solution.py:461
  16.3 1.5 %collective-permute-start.2 = (bf16[128,512]{1,0:T(8,128)(2,1)S(1)}, bf16[128,512]{1,0:T(8,128)(2,1)S(1)}, u32[]{:S(2)}, u32[]{:S(2)}) collective-permute-start(bf16[128,512]{1,0:T(8,128)(2,1)S(1)} %collective-permute-done.1.refs_4_), channel_id=1, source_target_pairs={{0,2},{2,0},{4,6},{6,4},{8,10},{10,8},{12,14},{14,12},{1,3},{3,1},... | collective-permute-start | bytes 393224 | tf_op jit(solution)/shard_map/ppermute | solution.py:461
  17.9 3.8 %prepare.1 = (bf16[4,128,512]{2,1,0:T(8,128)(2,1)}, bf16[32,128]{1,0:T(8,128)(2,1)}, bf16[128,2560]{1,0:T(8,128)(2,1)}, bf16[128,2560]{1,0:T(8,128)(2,1)}) custom-call(s32[1,8]{1,0:T(1,128)} %refs_1_.9, bf16[128,5120]{1,0:T(8,128)(2,1)} %bitcast.9, bf16[32,5120]{1,0:T(8,128)(2,1)} %bitcast.24, bf16[32,512]{1,0:T(8,128)(2,1)} %refs_12_.1, ...), custom_call_target="tpu_custom_call" | custom-call | flops 100000000 | bytes 6000000 | tf_op jit(solution)/shard_map/prepare/pallas_call | solution.py:117
  21.8 1.6 %collective-permute-done.4.refs_7_ = bf16[128,512]{1,0:T(8,128)(2,1)S(1)} collective-permute-done((bf16[128,512]{1,0:T(8,128)(2,1)S(1)}, bf16[128,512]{1,0:T(8,128)(2,1)S(1)}, u32[]{:S(2)}, u32[]{:S(2)}) %collective-permute-start.4) | collective-permute-done | bytes 131104 | tf_op jit(solution)/shard_map/ppermute | solution.py:461
  23.4 1.4 %collective-permute-done.2.refs_5_ = bf16[128,512]{1,0:T(8,128)(2,1)S(1)} collective-permute-done((bf16[128,512]{1,0:T(8,128)(2,1)S(1)}, bf16[128,512]{1,0:T(8,128)(2,1)S(1)}, u32[]{:S(2)}, u32[]{:S(2)}) %collective-permute-start.2) | collective-permute-done | bytes 131104 | tf_op jit(solution)/shard_map/ppermute | solution.py:461
  24.8 0.6 copy-done.16
  25.4 10.4 %stats.1 = (f32[8,32,128]{2,1,0:T(8,128)}, bf16[512,1024]{1,0:T(8,128)(2,1)}, f32[1,2560]{1,0:T(1,128)}) custom-call(s32[1,8]{1,0:T(1,128)} %refs_0_.9, s32[1,8]{1,0:T(1,128)} %refs_1_.9, bf16[128,512]{1,0:T(8,128)(2,1)} %bitcast.15, bf16[128,512]{1,0:T(8,128)(2,1)} %copy-done.10, bf16[128,512]{1,0:T(8,128)(2,1)} %copy-done.8, bf16[128,512]{1,0:T(8,128)(2,1)} %copy-done.16, ...), custom_call_target="tpu_custom_call" | custom-call | flops 2000000000 | bytes 5000000 | tf_op jit(solution)/shard_map/stats/pallas_call | solution.py:231
  35.9 13.5 %all_to_all.10.received_hbm = f32[8,32,128]{2,1,0:T(8,128)S(1)} all-to-all(f32[8,32,128]{2,1,0:T(8,128)} %get-tuple-element.36), channel_id=1, replica_groups=mesh['groups'=2,'node'=8,'rep'=2] {'node'}, dimensions={0} | all-to-all | bytes 262144 | tf_op jit(solution)/shard_map/all_to_all | solution.py:537
  49.3 1.2 %copy-done.18 = bf16[512,1024]{1,0:T(8,128)(2,1)S(1)} copy-done((bf16[512,1024]{1,0:T(8,128)(2,1)S(1)}, bf16[512,1024]{1,0:T(8,128)(2,1)}, u32[]{:S(2)}) %copy-start.18) | copy-done | bytes 1048600
  50.6 1.3 %gradients.1 = (f32[32,2816]{1,0:T(8,128)S(1)}, f32[32,2816]{1,0:T(8,128)S(1)}) custom-call(f32[8,32,128]{2,1,0:T(8,128)S(1)} %all_to_all.10.received_hbm, bf16[128,5120]{1,0:T(8,128)(2,1)S(1)} %bitcast.10, bf16[512,1024]{1,0:T(8,128)(2,1)S(1)} %copy-done.18, bf16[32,128]{1,0:T(8,128)(2,1)S(1)} %copy-done.21), custom_call_target="tpu_custom_call" | custom-call | flops 80000000 | bytes 4000000 | tf_op jit(solution)/shard_map/gradients/pallas_call | solution.py:398
  52.0 1.6 %collective-permute-done.8 = f32[32,2816]{1,0:T(8,128)S(1)} collective-permute-done((f32[32,2816]{1,0:T(8,128)S(1)}, f32[32,2816]{1,0:T(8,128)S(1)}, u32[]{:S(2)}, u32[]{:S(2)}) %collective-permute-start.8) | collective-permute-done | bytes 360480 | tf_op jit(solution)/shard_map/ppermute | solution.py:492
  53.9 0.3 collective-permute-start.9
  54.1 4.4 %collective-permute-done.9 = bf16[32,1408]{1,0:T(8,128)(2,1)S(1)} collective-permute-done((bf16[32,1408]{1,0:T(8,128)(2,1)S(1)}, bf16[32,1408]{1,0:T(8,128)(2,1)S(1)}, u32[]{:S(2)}, u32[]{:S(2)}) %collective-permute-start.9) | collective-permute-done | bytes 90144 | tf_op jit(solution)/shard_map/ppermute | solution.py:490
  58.7 3.7 %all-to-all-start = ((bf16[4,128,512]{2,1,0:T(8,128)(2,1)}), bf16[4,128,512]{2,1,0:T(8,128)(2,1)S(1)}, u32[]{:S(2)}, u32[]{:S(2)}) async-start(bf16[4,128,512]{2,1,0:T(8,128)(2,1)} %get-tuple-element.23), calls=%async_computation | async-start | bytes 1048576 | tf_op jit(solution)/shard_map/all_to_all | solution.py:478
  62.4 0.8 collective-permute-done.10
  63.2 1.9 %collective-permute-start.11 = (bf16[32,1408]{1,0:T(8,128)(2,1)S(1)}, bf16[32,1408]{1,0:T(8,128)(2,1)S(1)}, u32[]{:S(2)}, u32[]{:S(2)}) collective-permute-start(bf16[32,1408]{1,0:T(8,128)(2,1)S(1)} %add_convert_fusion.1), channel_id=1, source_target_pairs={{0,8},{2,10},{4,12},{6,14},{8,0},{10,2},{12,4},{14,6},{1,9},{3,11}... | collective-permute-start | bytes 270344 | tf_op jit(solution)/shard_map/ppermute | solution.py:490
  65.2 15.1 %collective-permute-done.11 = bf16[32,1408]{1,0:T(8,128)(2,1)S(1)} collective-permute-done((bf16[32,1408]{1,0:T(8,128)(2,1)S(1)}, bf16[32,1408]{1,0:T(8,128)(2,1)S(1)}, u32[]{:S(2)}, u32[]{:S(2)}) %collective-permute-start.11) | collective-permute-done | bytes 90144 | tf_op jit(solution)/shard_map/ppermute | solution.py:490
  80.3 1.1 collective-permute-start.12
  81.3 1.0 collective-permute-start.7
  82.4 3.5 %collective-permute-done.12 = bf16[32,1408]{1,0:T(8,128)(2,1)S(1)} collective-permute-done((bf16[32,1408]{1,0:T(8,128)(2,1)S(1)}, bf16[32,1408]{1,0:T(8,128)(2,1)S(1)}, u32[]{:S(2)}, u32[]{:S(2)}) %collective-permute-start.12) | collective-permute-done | bytes 90144 | tf_op jit(solution)/shard_map/ppermute | solution.py:490
  85.9 9.3 %collective-permute-done.7.refs_11_ = bf16[4,128,512]{2,1,0:T(8,128)(2,1)S(1)} collective-permute-done((bf16[4,128,512]{2,1,0:T(8,128)(2,1)S(1)}, bf16[4,128,512]{2,1,0:T(8,128)(2,1)S(1)}, u32[]{:S(2)}, u32[]{:S(2)}) %collective-permute-start.7) | collective-permute-done | bytes 524320 | tf_op jit(solution)/shard_map/ppermute | solution.py:481
  95.3 3.5 %attend.4 = (bf16[128,2560]{1,0:T(8,128)(2,1)}, bf16[128,2560]{1,0:T(8,128)(2,1)}) custom-call(s32[1,8]{1,0:T(1,128)S(1)} %copy-done.22, s32[1,8]{1,0:T(1,128)S(1)} %copy-done.20, bf16[128,512]{1,0:T(8,128)(2,1)S(1)} %bitcast.16, bf16[128,512]{1,0:T(8,128)(2,1)S(1)} %copy-done.11, bf16[128,512]{1,0:T(8,128)(2,1)S(1)} %copy-done.9, ...), custom_call_target="tpu_custom_call" | custom-call | flops 800000000 | bytes 1500000 | tf_op jit(solution)/shard_map/attend/pallas_call | solution.py:325
  98.8 3.5 %attend.5 = (bf16[128,2560]{1,0:T(8,128)(2,1)}, bf16[128,2560]{1,0:T(8,128)(2,1)}) custom-call(s32[1,8]{1,0:T(1,128)S(1)} %copy-done.22, s32[1,8]{1,0:T(1,128)S(1)} %copy-done.20, bf16[128,512]{1,0:T(8,128)(2,1)S(1)} %bitcast.17, bf16[128,512]{1,0:T(8,128)(2,1)S(1)} %copy-done.11, ...), custom_call_target="tpu_custom_call", output_to_operand_aliasing={{0}: (15, {}), {1}: (16, {})} | custom-call | flops 800000000 | bytes 1500000 | tf_op jit(solution)/shard_map/attend/pallas_call | solution.py:325
  102.3 3.5 %attend.6 = (bf16[128,2560]{1,0:T(8,128)(2,1)}, bf16[128,2560]{1,0:T(8,128)(2,1)}) custom-call(s32[1,8]{1,0:T(1,128)S(1)} %copy-done.22, s32[1,8]{1,0:T(1,128)S(1)} %copy-done.20, bf16[128,512]{1,0:T(8,128)(2,1)S(1)} %bitcast.18, bf16[128,512]{1,0:T(8,128)(2,1)S(1)} %copy-done.11, ...), custom_call_target="tpu_custom_call", output_to_operand_aliasing={{0}: (15, {}), {1}: (16, {})} | custom-call | flops 800000000 | bytes 1500000 | tf_op jit(solution)/shard_map/attend/pallas_call | solution.py:325
  105.7 3.5 %attend.7 = (bf16[128,2560]{1,0:T(8,128)(2,1)}, bf16[128,2560]{1,0:T(8,128)(2,1)}) custom-call(s32[1,8]{1,0:T(1,128)S(1)} %copy-done.22, s32[1,8]{1,0:T(1,128)S(1)} %copy-done.20, bf16[128,512]{1,0:T(8,128)(2,1)S(1)} %bitcast.19, bf16[128,512]{1,0:T(8,128)(2,1)S(1)} %copy-done.11, ...), custom_call_target="tpu_custom_call", output_to_operand_aliasing={{0}: (15, {}), {1}: (16, {})} | custom-call | flops 800000000 | bytes 1500000 | tf_op jit(solution)/shard_map/attend/pallas_call | solution.py:325
  109.2 0.9 finish.1
  (60 shorter events, 0.7 us)
Async XLA Ops:
  0.6 12.4 %collective-permute-start.5 = (bf16[128,512]{1,0:T(8,128)(2,1)}, bf16[128,512]{1,0:T(8,128)(2,1)S(1)}, u32[]{:S(2)}, u32[]{:S(2)}) collective-permute-start(bf16[128,512]{1,0:T(8,128)(2,1)} %bitcast.11), channel_id=1, source_target_pairs={{0,12},{2,14},{1,13},{3,15},{16,28},{18,30},{17,29},{19,31}} | collective-permute-start | bytes 393224 | tf_op jit(solution)/shard_map/ppermute | solution.py:457
  7.6 7.0 %collective-permute-start.3 = (bf16[128,512]{1,0:T(8,128)(2,1)}, bf16[128,512]{1,0:T(8,128)(2,1)S(1)}, u32[]{:S(2)}, u32[]{:S(2)}) collective-permute-start(bf16[128,512]{1,0:T(8,128)(2,1)} %bitcast.12), channel_id=1, source_target_pairs={{0,8},{2,10},{4,12},{6,14},{1,9},{3,11},{5,13},{7,15},{16,24},{18,... | collective-permute-start | bytes 393224 | tf_op jit(solution)/shard_map/ppermute | solution.py:457
  8.9 7.4 %collective-permute-start.1 = (bf16[128,512]{1,0:T(8,128)(2,1)}, bf16[128,512]{1,0:T(8,128)(2,1)S(1)}, u32[]{:S(2)}, u32[]{:S(2)}) collective-permute-start(bf16[128,512]{1,0:T(8,128)(2,1)} %bitcast.13), channel_id=1, source_target_pairs={{0,4},{2,6},{4,8},{6,10},{8,12},{10,14},{1,5},{3,7},{5,9},{7,11},{... | collective-permute-start | bytes 393224 | tf_op jit(solution)/shard_map/ppermute | solution.py:457
  11.4 10.3 %collective-permute-start = (bf16[128,512]{1,0:T(8,128)(2,1)}, bf16[128,512]{1,0:T(8,128)(2,1)S(1)}, u32[]{:S(2)}, u32[]{:S(2)}) collective-permute-start(bf16[128,512]{1,0:T(8,128)(2,1)} %bitcast.14), channel_id=1, source_target_pairs={{0,2},{2,0},{4,6},{6,4},{8,10},{10,8},{12,14},{14,12},{1,3},{3,1},... | collective-permute-start | bytes 393224 | tf_op jit(solution)/shard_map/ppermute | solution.py:461
  13.0 8.7 %copy-start.4 = (bf16[128,512]{1,0:T(8,128)(2,1)}, bf16[128,512]{1,0:T(8,128)(2,1)S(1)}, u32[]{:S(2)}) copy-start(bf16[128,512]{1,0:T(8,128)(2,1)S(1)} %collective-permute-done.5.refs_8_) | copy-start | bytes 393220
  13.0 8.7 %collective-permute-start.6 = (bf16[128,512]{1,0:T(8,128)(2,1)S(1)}, bf16[128,512]{1,0:T(8,128)(2,1)S(1)}, u32[]{:S(2)}, u32[]{:S(2)}) collective-permute-start(bf16[128,512]{1,0:T(8,128)(2,1)S(1)} %collective-permute-done.5.refs_8_), channel_id=1, source_target_pairs={{0,2},{2,0},{4,6},{6,4},{8,10},{10,8},{12,14},{14,12},{1,3},{3,1},... | collective-permute-start | bytes 393224 | tf_op jit(solution)/shard_map/ppermute | solution.py:461
  14.7 7.1 %copy-start.6 = (bf16[128,512]{1,0:T(8,128)(2,1)}, bf16[128,512]{1,0:T(8,128)(2,1)S(1)}, u32[]{:S(2)}) copy-start(bf16[128,512]{1,0:T(8,128)(2,1)S(1)} %collective-permute-done.3.refs_6_) | copy-start | bytes 393220
  14.7 8.7 %collective-permute-start.4 = (bf16[128,512]{1,0:T(8,128)(2,1)S(1)}, bf16[128,512]{1,0:T(8,128)(2,1)S(1)}, u32[]{:S(2)}, u32[]{:S(2)}) collective-permute-start(bf16[128,512]{1,0:T(8,128)(2,1)S(1)} %collective-permute-done.3.refs_6_), channel_id=1, source_target_pairs={{0,2},{2,0},{4,6},{6,4},{8,10},{10,8},{12,14},{14,12},{1,3},{3,1},... | collective-permute-start | bytes 393224 | tf_op jit(solution)/shard_map/ppermute | solution.py:461
  16.3 8.5 %collective-permute-start.2 = (bf16[128,512]{1,0:T(8,128)(2,1)S(1)}, bf16[128,512]{1,0:T(8,128)(2,1)S(1)}, u32[]{:S(2)}, u32[]{:S(2)}) collective-permute-start(bf16[128,512]{1,0:T(8,128)(2,1)S(1)} %collective-permute-done.1.refs_4_), channel_id=1, source_target_pairs={{0,2},{2,0},{4,6},{6,4},{8,10},{10,8},{12,14},{14,12},{1,3},{3,1},... | collective-permute-start | bytes 393224 | tf_op jit(solution)/shard_map/ppermute | solution.py:461
  25.4 23.9 %copy-start.2 = (bf16[1,128,5120]{2,1,0:T(8,128)(2,1)S(1)}, bf16[1,128,5120]{2,1,0:T(8,128)(2,1)}, u32[]{:S(2)}) copy-start(bf16[1,128,5120]{2,1,0:T(8,128)(2,1)} %param.9) | copy-start | bytes 3932164
  25.4 23.9 %copy-start.21 = (bf16[32,128]{1,0:T(8,128)(2,1)S(1)}, bf16[32,128]{1,0:T(8,128)(2,1)}, u32[]{:S(2)}) copy-start(bf16[32,128]{1,0:T(8,128)(2,1)} %get-tuple-element.26.refs_13_.low_ref) | copy-start | bytes 24580
  51.9 1.7 %collective-permute-start.8 = (f32[32,2816]{1,0:T(8,128)S(1)}, f32[32,2816]{1,0:T(8,128)S(1)}, u32[]{:S(2)}, u32[]{:S(2)}) collective-permute-start(f32[32,2816]{1,0:T(8,128)S(1)} %get-tuple-element.39), channel_id=1, source_target_pairs={{0,1},{1,0},{2,3},{3,2},{4,5},{5,4},{6,7},{7,6},{8,9},{9,8},{10,11... | collective-permute-start | bytes 1081352 | tf_op jit(solution)/shard_map/ppermute | solution.py:492
  53.7 41.5 %copy-start = (bf16[128,2560]{1,0:T(8,128)(2,1)S(1)}, bf16[128,2560]{1,0:T(8,128)(2,1)}, u32[]{:S(2)}) copy-start(bf16[128,2560]{1,0:T(8,128)(2,1)} %get-tuple-element.24.refs_10_.refs_12_) | copy-start | bytes 1966084
  53.7 41.5 %copy-start.1 = (bf16[128,2560]{1,0:T(8,128)(2,1)S(1)}, bf16[128,2560]{1,0:T(8,128)(2,1)}, u32[]{:S(2)}) copy-start(bf16[128,2560]{1,0:T(8,128)(2,1)} %get-tuple-element.25.refs_11_.refs_13_) | copy-start | bytes 1966084
  53.7 41.5 %copy-start.3 = (bf16[1,128,512]{2,1,0:T(8,128)(2,1)S(1)}, bf16[1,128,512]{2,1,0:T(8,128)(2,1)}, u32[]{:S(2)}) copy-start(bf16[1,128,512]{2,1,0:T(8,128)(2,1)} %param.11) | copy-start | bytes 393220
  53.8 41.5 %copy-start.5 = (bf16[128,512]{1,0:T(8,128)(2,1)S(1)}, bf16[128,512]{1,0:T(8,128)(2,1)}, u32[]{:S(2)}) copy-start(bf16[128,512]{1,0:T(8,128)(2,1)} %copy-done.4) | copy-start | bytes 393220
  53.8 41.5 %copy-start.7 = (bf16[128,512]{1,0:T(8,128)(2,1)S(1)}, bf16[128,512]{1,0:T(8,128)(2,1)}, u32[]{:S(2)}) copy-start(bf16[128,512]{1,0:T(8,128)(2,1)} %copy-done.6) | copy-start | bytes 393220
  53.8 41.5 %copy-start.9 = (bf16[128,512]{1,0:T(8,128)(2,1)S(1)}, bf16[128,512]{1,0:T(8,128)(2,1)}, u32[]{:S(2)}) copy-start(bf16[128,512]{1,0:T(8,128)(2,1)} %copy-done.8) | copy-start | bytes 393220
  53.8 41.5 %copy-start.11 = (bf16[128,512]{1,0:T(8,128)(2,1)S(1)}, bf16[128,512]{1,0:T(8,128)(2,1)}, u32[]{:S(2)}) copy-start(bf16[128,512]{1,0:T(8,128)(2,1)} %copy-done.10) | copy-start | bytes 393220
  53.8 41.5 %copy-start.13 = (bf16[128,512]{1,0:T(8,128)(2,1)S(1)}, bf16[128,512]{1,0:T(8,128)(2,1)}, u32[]{:S(2)}) copy-start(bf16[128,512]{1,0:T(8,128)(2,1)} %copy-done.12) | copy-start | bytes 393220
  53.8 41.5 %copy-start.15 = (bf16[128,512]{1,0:T(8,128)(2,1)S(1)}, bf16[128,512]{1,0:T(8,128)(2,1)}, u32[]{:S(2)}) copy-start(bf16[128,512]{1,0:T(8,128)(2,1)} %copy-done.14) | copy-start | bytes 393220
  53.8 41.5 %copy-start.17 = (bf16[128,512]{1,0:T(8,128)(2,1)S(1)}, bf16[128,512]{1,0:T(8,128)(2,1)}, u32[]{:S(2)}) copy-start(bf16[128,512]{1,0:T(8,128)(2,1)} %copy-done.16) | copy-start | bytes 393220
  53.8 41.5 %copy-start.19 = (f32[1,2560]{1,0:T(1,128)S(1)}, f32[1,2560]{1,0:T(1,128)}, u32[]{:S(2)}) copy-start(f32[1,2560]{1,0:T(1,128)} %get-tuple-element.27.refs_14_) | copy-start | bytes 30724
  53.8 41.5 %copy-start.20 = (s32[1,8]{1,0:T(1,128)S(1)}, s32[1,8]{1,0:T(1,128)}, u32[]{:S(2)}) copy-start(s32[1,8]{1,0:T(1,128)} %refs_1_.9) | copy-start | bytes 100
  53.8 41.4 %copy-start.22 = (s32[1,8]{1,0:T(1,128)S(1)}, s32[1,8]{1,0:T(1,128)}, u32[]{:S(2)}) copy-start(s32[1,8]{1,0:T(1,128)} %refs_0_.9) | copy-start | bytes 100
  53.9 4.7 %collective-permute-start.9 = (bf16[32,1408]{1,0:T(8,128)(2,1)S(1)}, bf16[32,1408]{1,0:T(8,128)(2,1)S(1)}, u32[]{:S(2)}, u32[]{:S(2)}) collective-permute-start(bf16[32,1408]{1,0:T(8,128)(2,1)S(1)} %select_convert_fusion), channel_id=1, source_target_pairs={{0,2},{2,0},{4,6},{6,4},{8,10},{10,8},{12,14},{14,12},{1,3},{3,1},... | collective-permute-start | bytes 270344 | tf_op jit(solution)/shard_map/ppermute | solution.py:490
  58.6 4.6 %collective-permute-start.10 = (bf16[32,1408]{1,0:T(8,128)(2,1)S(1)}, bf16[32,1408]{1,0:T(8,128)(2,1)S(1)}, u32[]{:S(2)}, u32[]{:S(2)}) collective-permute-start(bf16[32,1408]{1,0:T(8,128)(2,1)S(1)} %add_convert_fusion.2), channel_id=1, source_target_pairs={{0,4},{2,6},{4,0},{6,2},{8,12},{10,14},{12,8},{14,10},{1,5},{3,7},... | collective-permute-start | bytes 270344 | tf_op jit(solution)/shard_map/ppermute | solution.py:490
  58.7 22.6 %all-to-all-start = ((bf16[4,128,512]{2,1,0:T(8,128)(2,1)}), bf16[4,128,512]{2,1,0:T(8,128)(2,1)S(1)}, u32[]{:S(2)}, u32[]{:S(2)}) async-start(bf16[4,128,512]{2,1,0:T(8,128)(2,1)} %get-tuple-element.23), calls=%async_computation | async-start | bytes 1048576 | tf_op jit(solution)/shard_map/all_to_all | solution.py:478
  63.2 17.0 %collective-permute-start.11 = (bf16[32,1408]{1,0:T(8,128)(2,1)S(1)}, bf16[32,1408]{1,0:T(8,128)(2,1)S(1)}, u32[]{:S(2)}, u32[]{:S(2)}) collective-permute-start(bf16[32,1408]{1,0:T(8,128)(2,1)S(1)} %add_convert_fusion.1), channel_id=1, source_target_pairs={{0,8},{2,10},{4,12},{6,14},{8,0},{10,2},{12,4},{14,6},{1,9},{3,11}... | collective-permute-start | bytes 270344 | tf_op jit(solution)/shard_map/ppermute | solution.py:490
  80.3 5.6 %collective-permute-start.12 = (bf16[32,1408]{1,0:T(8,128)(2,1)S(1)}, bf16[32,1408]{1,0:T(8,128)(2,1)S(1)}, u32[]{:S(2)}, u32[]{:S(2)}) collective-permute-start(bf16[32,1408]{1,0:T(8,128)(2,1)S(1)} %add_convert_fusion), channel_id=1, source_target_pairs={{0,2},{2,0},{4,6},{6,4},{8,10},{10,8},{12,14},{14,12},{1,3},{3,1},... | collective-permute-start | bytes 270344 | tf_op jit(solution)/shard_map/ppermute | solution.py:490
  81.3 13.9 %collective-permute-start.7 = (bf16[4,128,512]{2,1,0:T(8,128)(2,1)S(1)}, bf16[4,128,512]{2,1,0:T(8,128)(2,1)S(1)}, u32[]{:S(2)}, u32[]{:S(2)}) collective-permute-start(bf16[4,128,512]{2,1,0:T(8,128)(2,1)S(1)} %all-to-all-done.refs_10_), channel_id=1, source_target_pairs={{0,2},{2,0},{4,6},{6,4},{8,10},{10,8},{12,14},{14,12},{1,3},{3,1},... | collective-permute-start | bytes 1572872 | tf_op jit(solution)/shard_map/ppermute | solution.py:481
  85.9 23.4 %collective-permute-start.13 = (bf16[32,2816]{1,0:T(8,128)(2,1)S(1)}, bf16[32,2816]{1,0:T(8,128)(2,1)S(1)}, u32[]{:S(2)}, u32[]{:S(2)}) collective-permute-start(bf16[32,2816]{1,0:T(8,128)(2,1)S(1)} %pad_maximum_fusion.half_ref), channel_id=1, source_target_pairs={{0,1},{1,0},{2,3},{3,2},{4,5},{5,4},{6,7},{7,6},{8,9},{9,8},{10,11... | collective-permute-start | bytes 540680 | tf_op jit(solution)/shard_map/ppermute | solution.py:506
  (6 other events, 14.8 us)
